TPU v7x, 256 devices: a whole 4x4x8 slice. The times are simulated.
256 devices in a mesh: group: 4 (over y_lo, core), inner: 64 (over x, z, y_hi).
Axes of the slice: x: 4, y: 4 (y_hi: 2, y_lo: 2; y = y_hi * 2 + y_lo), z: 8, core: 2. Of those that a mesh axis runs over, the one named last changes fastest.
Arguments:
- tokens: bfloat16 [256, 196, 1024], P('inner'), may hold values from -128 to 128
- output_grad: bfloat16 [256, 196, 1024], P('inner'), may hold values from -6 to 6
- router: bfloat16 [1024, 128], replicated, may hold values from -0.1890625 to 0.1890625
- weight_in: bfloat16 [128, 1024, 4096], P('inner', None, 'group'), may hold values from -0.1875 to 0.1875
- weight_out: bfloat16 [128, 4096, 1024], P('inner', 'group'), may hold values from -0.09375 to 0.09375
Outputs:
- token_grad: bfloat16 [256, 196, 1024], P('inner', None, 'group')
- router_grad: float32 [1024, 128], P('inner')
All inputs are finite; a program needn't handle non-finite values.
Results may differ from a plain program's by a relative error of at most 0.015.
Values may be sent and summed in bfloat16 or wider, within the bound.
A program may use at most 64 MiB of HBM per device.

v0:
```python
import jax
import jax.numpy as jnp
from jax import lax
from jax.sharding import PartitionSpec as P


def in_one_piece(arrays, axis, split_dim, concat_dim, along):
    widths = [a.shape[along] for a in arrays]
    both = jnp.concatenate(arrays, axis=along)
    out = lax.all_to_all(both, axis, split_axis=split_dim, concat_axis=concat_dim, tiled=True)
    return tuple(jnp.split(out, [sum(widths[:k]) for k in range(1, len(widths))], axis=along))


def cut_along(value, dim, size):
    dims = value.shape
    tiles = value.reshape(*dims[:dim], size, dims[dim] // size, *dims[dim + 1 :])
    return jnp.moveaxis(tiles, dim, 0)


def summed_on_arrival(value, axis, dim):
    size = lax.axis_size(axis)
    tiles = lax.all_to_all(cut_along(value, dim, size), axis, 0, 0, tiled=True)
    return jnp.sum(tiles.astype(jnp.float32), axis=0)


def in_one_piece_2(arrays, axis, dim, along):
    widths = [a.shape[along] for a in arrays]
    both = jnp.concatenate(arrays, axis=along)
    out = summed_on_arrival(both, axis, dim)
    return tuple(jnp.split(out, [sum(widths[:k]) for k in range(1, len(widths))], axis=along))


def sent_to_all(value, axis):
    copies = jnp.broadcast_to(value, (lax.axis_size(axis), *value.shape))
    return lax.all_to_all(copies, axis, split_axis=0, concat_axis=0, tiled=True)


def of_everyone(value, axis):
    everything = sent_to_all(value, axis)
    return jnp.sum(everything.astype(jnp.float32), axis=0)


def local(tokens, output_grad, router, weight_in, weight_out):
    logits = jnp.einsum("bmd,ds->bms", tokens, router, preferred_element_type=jnp.float32)
    dispatch = jax.nn.softmax(logits, axis=1)
    combine = jax.nn.softmax(logits, axis=2)
    dispatch_b = dispatch.astype(jnp.bfloat16)
    combine_b = combine.astype(jnp.bfloat16)
    slot_in = jnp.einsum(
        "bms,bmd->bsd", dispatch_b, tokens, preferred_element_type=jnp.float32
    ).astype(jnp.bfloat16)
    slot_grad = jnp.einsum(
        "bms,bmd->bsd", combine_b, output_grad, preferred_element_type=jnp.float32
    ).astype(jnp.bfloat16)
    expert_x, expert_g = in_one_piece((slot_in, slot_grad), "inner", 1, 0, 2)
    pre_act = jnp.einsum("bed,edf->ebf", expert_x, weight_in, preferred_element_type=jnp.float32)
    activated, gelu_back = jax.vjp(jax.nn.gelu, pre_act)
    out_part = jnp.einsum(
        "ebf,efd->bed",
        activated.astype(jnp.bfloat16),
        weight_out,
        preferred_element_type=jnp.float32,
    )
    act_grad = jnp.einsum("bed,efd->ebf", expert_g, weight_out, preferred_element_type=jnp.float32)
    pre_grad = gelu_back(act_grad)[0].astype(jnp.bfloat16)
    back_part = jnp.einsum("ebf,edf->bed", pre_grad, weight_in, preferred_element_type=jnp.float32)
    feature_width = tokens.shape[2] // lax.axis_size("group")
    offset = lax.axis_index("group") * feature_width
    router_piece = lax.dynamic_slice_in_dim(router, offset, feature_width, 0)
    out_share, back_share = in_one_piece_2(
        (out_part.astype(jnp.bfloat16), back_part.astype(jnp.bfloat16)), "group", 2, 0
    )
    slot_out, back_piece = in_one_piece(
        (out_share.astype(jnp.bfloat16), back_share.astype(jnp.bfloat16)), "inner", 0, 1, 2
    )
    grad_piece = lax.dynamic_slice_in_dim(output_grad, offset, feature_width, 2)
    token_piece = lax.dynamic_slice_in_dim(tokens, offset, feature_width, 2)
    combine_part = jnp.einsum(
        "bmd,bsd->bms", grad_piece, slot_out, preferred_element_type=jnp.float32
    )
    dispatch_part = jnp.einsum(
        "bmd,bsd->bms", token_piece, back_piece, preferred_element_type=jnp.float32
    )
    combine_grad, dispatch_grad = (
        of_everyone(combine_part.astype(jnp.bfloat16), "group").astype(jnp.float32),
        of_everyone(dispatch_part.astype(jnp.bfloat16), "group").astype(jnp.float32),
    )
    logit_grad = combine * (combine_grad - jnp.sum(combine * combine_grad, axis=2, keepdims=True))
    logit_grad = logit_grad + dispatch * (
        dispatch_grad - jnp.sum(dispatch * dispatch_grad, axis=1, keepdims=True)
    )
    logit_b = logit_grad.astype(jnp.bfloat16)
    token_grad = jnp.einsum(
        "bms,bsd->bmd", dispatch_b, back_piece, preferred_element_type=jnp.float32
    )
    token_grad = token_grad + jnp.einsum(
        "bms,ds->bmd", logit_b, router_piece, preferred_element_type=jnp.float32
    )
    router_grad = summed_on_arrival(
        jnp.einsum("bmd,bms->ds", tokens, logit_b, preferred_element_type=jnp.float32).astype(
            jnp.bfloat16
        ),
        "inner",
        0,
    )
    return (token_grad.astype(jnp.bfloat16), router_grad)


def solution(mesh):
    return jax.shard_map(
        local,
        mesh=mesh,
        in_specs=(
            P("inner", None, None),
            P("inner", None, None),
            P(),
            P("inner", None, "group"),
            P("inner", "group", None),
        ),
        out_specs=(P("inner", None, "group"), P("inner", None)),
        check_vma=False,
    )
```

profile of v0, /device:TPU:1, one launch (start us, length us, event | category | flops | bytes accessed | tf_op | source)
XLA Modules:
  0.0 214.8 jit_solution(17097976402249709328)
XLA Ops:
  0.6 0.0 copy-start
  0.6 0.9 copy-done
  1.6 2.4 %fusion.57 = f32[4,196,128]{2,1,0:T(8,128)S(1)} fusion(bf16[1024,128]{1,0:T(8,128)(2,1)S(1)} %copy-done, bf16[4,196,1024]{2,0,1:T(4,128)(2,1)} %param.5), kind=kOutput, calls=%fused_computation.69 | convolution fusion | flops 205520896 | bytes 2269184 | tf_op jit(solution)/shard_map/bmd,ds->bms/dot_general | solution.py:44
  4.0 0.9 fusion.88
  4.9 0.9 fusion.87
  5.8 0.0 copy-start.2
  5.8 2.8 %convolution_convert_fusion.3 = bf16[4,128,1024]{2,1,0:T(8,128)(2,1)S(1)} fusion(bf16[4,196,1024]{2,0,1:T(4,128)(2,1)} %param.5, f32[4,128]{1,0:T(4,128)S(1)} %get-tuple-element.14, f32[4,196,128]{2,1,0:T(8,128)S(1)} %fusion.57), kind=kOutput, calls=%fused_computation.23 | convolution fusion | flops 206346944 | bytes 3057664 | tf_op jit(solution)/shard_map/bms,bmd->bsd/dot_general | solution.py:49
  8.6 0.0 copy-done.2
  8.6 3.4 %convolution_convert_fusion.2 = bf16[4,128,1024]{2,1,0:T(8,128)(2,1)} fusion(f32[4,196]{1,0:T(4,128)S(1)} %get-tuple-element.12, f32[4,196,128]{2,1,0:T(8,128)S(1)} %fusion.57, bf16[4,196,1024]{2,0,1:T(4,128)(2,1)S(1)} %copy-done.2), kind=kOutput, calls=%fused_computation.22 | convolution fusion | flops 206347152 | bytes 3058752 | tf_op jit(solution)/shard_map/bms,bmd->bsd/dot_general | solution.py:52
  12.0 1.4 pad_maximum_fusion
  13.4 1.6 copy.44
  15.0 66.1 %all_to_all.56 = bf16[4,128,2048]{2,0,1:T(4,128)(2,1)S(1)} all-to-all(bf16[4,128,2048]{2,0,1:T(4,128)(2,1)S(1)} %copy.44), channel_id=1, replica_groups=mesh['group'=4,'inner'=64] {'inner'}, dimensions={1} | all-to-all | bytes 4194304 | tf_op jit(solution)/shard_map/all_to_all | solution.py:10
  81.1 1.2 copy.98
  82.3 2.1 all_to_all.41
  84.3 0.0 copy-start.1
  84.3 5.3 %fusion.33 = f32[2,256,1024]{2,1,0:T(8,128)} fusion(bf16[2,1024,1024]{2,1,0:T(8,128)(2,1)} %param.8, bf16[256,2,2048]{2,0,1:T(8,128)(2,1)} %all_to_all.41), kind=kOutput, calls=%fused_computation.45 | convolution fusion | flops 1073741824 | bytes 7340032 | tf_op jit(solution)/shard_map/bed,edf->ebf/dot_general | solution.py:56
  89.6 0.0 copy-done.1
  89.6 8.0 %fusion.12 = bf16[256,2,1024]{2,0,1:T(8,128)(2,1)} fusion(bf16[2,1024,1024]{2,1,0:T(8,128)(2,1)} %param.8, f32[2,256,1024]{2,1,0:T(8,128)} %fusion.33, bf16[2,1024,1024]{2,1,0:T(8,128)(2,1)} %param.9, bf16[256,2,2048]{2,0,1:T(8,128)(2,1)S(1)} %copy-done.1), kind=kOutput, calls=%fused_computation.25 | convolution fusion | flops 2158493696 | bytes 12582912 | tf_op jit(solution)/shard_map/ebf,edf->bed/dot_general | solution.py:66
  97.6 0.0 copy-start.3
  97.6 4.3 %fusion.11 = bf16[256,2,1024]{2,0,1:T(8,128)(2,1)S(1)} fusion(bf16[2,1024,1024]{2,1,0:T(8,128)(2,1)} %param.9, f32[2,256,1024]{2,1,0:T(8,128)} %fusion.33), kind=kOutput, calls=%fused_computation.24 | convolution fusion | flops 1078984704 | bytes 7340032 | tf_op jit(solution)/shard_map/ebf,efd->bed/dot_general | solution.py:58
  101.9 0.0 copy-done.3
  101.9 0.2 pad_maximum_fusion.1
  102.1 0.1 copy.97
  102.3 29.8 %all_to_all.57 = bf16[4,512,2,256]{3,1,2,0:T(8,128)(2,1)S(1)} all-to-all(bf16[4,512,2,256]{3,1,2,0:T(8,128)(2,1)S(1)} %bitcast.47), channel_id=1, replica_groups=mesh['group'=4,'inner'=64] {'group'}, dimensions={0} | all-to-all | bytes 4194304 | tf_op jit(solution)/shard_map/all_to_all | solution.py:22
  132.1 0.6 reduce
  132.9 1.3 copy.48
  134.2 5.6 %all-to-all-start.2 = ((bf16[256,2,512]{2,1,0:T(2,128)(2,1)}), bf16[256,2,512]{2,1,0:T(2,128)(2,1)S(1)}, u32[]{:S(2)}, u32[]{:S(2)}) async-start(bf16[256,2,512]{2,1,0:T(2,128)(2,1)} %copy.48), calls=%async_computation.2 | async-start | bytes 1048576 | tf_op jit(solution)/shard_map/all_to_all | solution.py:10
  139.8 1.9 copy.43
  141.7 15.1 %all-to-all-done.2 = bf16[256,2,512]{2,1,0:T(2,128)(2,1)S(1)} async-done(((bf16[256,2,512]{2,1,0:T(2,128)(2,1)}), bf16[256,2,512]{2,1,0:T(2,128)(2,1)S(1)}, u32[]{:S(2)}, u32[]{:S(2)}) %all-to-all-start.2) | async-done | bytes 524320 | tf_op jit(solution)/shard_map/all_to_all | solution.py:10
  156.8 0.4 copy.49
  157.2 0.2 all_to_all.46
  157.4 0.3 convolution_convert_fusion.5
  157.7 0.1 copy.51
  157.8 1.1 broadcast_in_dim.4
  158.9 6.6 %all-to-all-start.3 = ((bf16[4,4,196,128]{3,1,2,0:T(4,128)(2,1)}), bf16[4,4,196,128]{3,1,2,0:T(4,128)(2,1)S(1)}, u32[]{:S(2)}, u32[]{:S(2)}) async-start(bf16[4,4,196,128]{3,1,2,0:T(4,128)(2,1)} %broadcast_in_dim.4), calls=%async_computation.3 | async-start | bytes 1605632 | tf_op jit(solution)/shard_map/all_to_all | solution.py:35
  165.5 1.9 copy.41
  167.4 0.3 convolution_convert_fusion.4
  167.7 0.0 copy-start.4
  167.7 0.1 copy.55
  167.8 8.5 %all-to-all-done.3 = bf16[4,4,196,128]{3,1,2,0:T(4,128)(2,1)S(1)} async-done(((bf16[4,4,196,128]{3,1,2,0:T(4,128)(2,1)}), bf16[4,4,196,128]{3,1,2,0:T(4,128)(2,1)S(1)}, u32[]{:S(2)}, u32[]{:S(2)}) %all-to-all-start.3) | async-done | bytes 802848 | tf_op jit(solution)/shard_map/all_to_all | solution.py:35
  176.3 1.1 broadcast_in_dim.5
  177.4 4.4 %all-to-all-start.4 = ((bf16[4,4,196,128]{3,1,2,0:T(4,128)(2,1)}), bf16[4,4,196,128]{3,1,2,0:T(4,128)(2,1)S(1)}, u32[]{:S(2)}, u32[]{:S(2)}) async-start(bf16[4,4,196,128]{3,1,2,0:T(4,128)(2,1)} %broadcast_in_dim.5), calls=%async_computation.4 | async-start | bytes 1605632 | tf_op jit(solution)/shard_map/all_to_all | solution.py:35
  181.9 0.4 convert_reduce_fusion.1
  182.2 0.0 copy-done.4
  182.2 5.0 %fusion.22 = f32[4,196,128]{2,1,0:T(8,128)} fusion(f32[4,196,128]{2,0,1:T(4,128)S(1)} %convert_reduce_fusion.1, f32[4,196,128]{2,1,0:T(8,128)S(1)} %copy-done.4, f32[4,196]{1,0:T(4,128)S(1)} %get-tuple-element.12), kind=kOutput, calls=%fused_computation.37 | output fusion | flops 502671 | bytes 1207360 | tf_op jit(solution)/shard_map/sub | solution.py:88
  187.3 5.4 %all-to-all-done.4 = bf16[4,4,196,128]{3,1,2,0:T(4,128)(2,1)S(1)} async-done(((bf16[4,4,196,128]{3,1,2,0:T(4,128)(2,1)}), bf16[4,4,196,128]{3,1,2,0:T(4,128)(2,1)S(1)}, u32[]{:S(2)}, u32[]{:S(2)}) %all-to-all-start.4) | async-done | bytes 802848 | tf_op jit(solution)/shard_map/all_to_all | solution.py:35
  192.7 0.4 convert_reduce_fusion
  193.1 3.0 %fusion.25 = bf16[1024,128]{0,1:T(8,128)(2,1)S(1)} fusion(f32[4,196,128]{2,1,0:T(8,128)} %fusion.22, f32[4,196,128]{2,0,1:T(4,128)S(1)} %convert_reduce_fusion, bf16[4,196,1024]{2,0,1:T(4,128)(2,1)} %param.5, f32[4,196,128]{2,1,0:T(8,128)} %get-tuple-element.15, f32[4,128]{1,0:T(4,128)S(1)} %get-tuple-element.14), kind=kOutput, calls=%fused_computation.42 | convolution fusion | flops 206355136 | bytes 3074048 | tf_op jit(solution)/shard_map/bmd,bms->ds/dot_general | solution.py:100
  196.1 0.0 copy-start.5
  196.1 0.8 copy.59
  197.0 5.7 %all-to-all-start.5 = ((bf16[64,16,128]{2,1,0:T(8,128)(2,1)}), bf16[64,16,128]{2,1,0:T(8,128)(2,1)S(1)}, u32[]{:S(2)}, u32[]{:S(2)}) async-start(bf16[64,16,128]{2,1,0:T(8,128)(2,1)} %bitcast.11), calls=%async_computation.5 | async-start | bytes 524288 | tf_op jit(solution)/shard_map/all_to_all | solution.py:22
  202.6 0.3 fusion.60
  202.9 0.0 copy-done.5
  202.9 1.5 fusion.13
  204.4 0.9 copy.60
  205.3 8.8 %all-to-all-done.5 = bf16[64,16,128]{2,1,0:T(8,128)(2,1)S(1)} async-done(((bf16[64,16,128]{2,1,0:T(8,128)(2,1)}), bf16[64,16,128]{2,1,0:T(8,128)(2,1)S(1)}, u32[]{:S(2)}, u32[]{:S(2)}) %all-to-all-start.5) | async-done | bytes 262176 | tf_op jit(solution)/shard_map/all_to_all | solution.py:22
  214.1 0.7 convert_reduce_fusion.2
  (2 shorter events, 0.1 us)
Async XLA Ops:
  0.6 1.0 copy-start
  5.8 2.8 %copy-start.2 = (bf16[4,196,1024]{2,0,1:T(4,128)(2,1)S(1)}, bf16[4,196,1024]{2,0,1:T(4,128)(2,1)}, u32[]{:S(2)}) copy-start(bf16[4,196,1024]{2,0,1:T(4,128)(2,1)} %param.6) | copy-start | bytes 4816900
  84.3 5.3 %copy-start.1 = (bf16[256,2,2048]{2,0,1:T(8,128)(2,1)S(1)}, bf16[256,2,2048]{2,0,1:T(8,128)(2,1)}, u32[]{:S(2)}) copy-start(bf16[256,2,2048]{2,0,1:T(8,128)(2,1)} %all_to_all.41) | copy-start | bytes 6291460
  97.6 4.3 %copy-start.3 = (bf16[256,2,1024]{2,0,1:T(8,128)(2,1)S(1)}, bf16[256,2,1024]{2,0,1:T(8,128)(2,1)}, u32[]{:S(2)}) copy-start(bf16[256,2,1024]{2,0,1:T(8,128)(2,1)} %fusion.12) | copy-start | bytes 3145732
  134.2 22.6 %all-to-all-start.2 = ((bf16[256,2,512]{2,1,0:T(2,128)(2,1)}), bf16[256,2,512]{2,1,0:T(2,128)(2,1)S(1)}, u32[]{:S(2)}, u32[]{:S(2)}) async-start(bf16[256,2,512]{2,1,0:T(2,128)(2,1)} %copy.48), calls=%async_computation.2 | async-start | bytes 1048576 | tf_op jit(solution)/shard_map/all_to_all | solution.py:10
  158.9 17.4 %all-to-all-start.3 = ((bf16[4,4,196,128]{3,1,2,0:T(4,128)(2,1)}), bf16[4,4,196,128]{3,1,2,0:T(4,128)(2,1)S(1)}, u32[]{:S(2)}, u32[]{:S(2)}) async-start(bf16[4,4,196,128]{3,1,2,0:T(4,128)(2,1)} %broadcast_in_dim.4), calls=%async_computation.3 | async-start | bytes 1605632 | tf_op jit(solution)/shard_map/all_to_all | solution.py:35
  167.7 14.5 %copy-start.4 = (f32[4,196,128]{2,1,0:T(8,128)S(1)}, f32[4,196,128]{2,1,0:T(8,128)}, u32[]{:S(2)}) copy-start(f32[4,196,128]{2,1,0:T(8,128)} %get-tuple-element.13) | copy-start | bytes 1204228
  177.4 15.3 %all-to-all-start.4 = ((bf16[4,4,196,128]{3,1,2,0:T(4,128)(2,1)}), bf16[4,4,196,128]{3,1,2,0:T(4,128)(2,1)S(1)}, u32[]{:S(2)}, u32[]{:S(2)}) async-start(bf16[4,4,196,128]{3,1,2,0:T(4,128)(2,1)} %broadcast_in_dim.5), calls=%async_computation.4 | async-start | bytes 1605632 | tf_op jit(solution)/shard_map/all_to_all | solution.py:35
  196.1 6.8 %copy-start.5 = (f32[4,196,128]{2,1,0:T(8,128)S(1)}, f32[4,196,128]{2,1,0:T(8,128)}, u32[]{:S(2)}) copy-start(f32[4,196,128]{2,1,0:T(8,128)} %fusion.22) | copy-start | bytes 1204228
  197.0 17.2 %all-to-all-start.5 = ((bf16[64,16,128]{2,1,0:T(8,128)(2,1)}), bf16[64,16,128]{2,1,0:T(8,128)(2,1)S(1)}, u32[]{:S(2)}, u32[]{:S(2)}) async-start(bf16[64,16,128]{2,1,0:T(8,128)(2,1)} %bitcast.11), calls=%async_computation.5 | async-start | bytes 524288 | tf_op jit(solution)/shard_map/all_to_all | solution.py:22
where the time goes:
time: 217 us; the launch traced here: 215 us
  blocking collectives  95.9 us (44%)
  waiting for transfers between devices  37.9 us (17%)
  matrix products  31.5 us (15%)
  starting transfers between devices  22.3 us (10%)
  local copies, waits for them, and re-layouts  15.8 us (7%)
  other arithmetic  10.5 us (5%)
    all_to_all x1, blocking collectives, in_one_piece(): lax.all_to_all(both, axis, split_axis=split_dim, concat_axis=concat_dim,...  66.1 us
    all_to_all x1, blocking collectives, summed_on_arrival(): tiles = lax.all_to_all(cut_along(value, dim, size), axis, 0, 0, tiled=True)  29.8 us
    all_to_all x1, waiting for transfers between devices, in_one_piece(): lax.all_to_all(both, axis, split_axis=split_dim, concat_axis=concat_dim,...  15.1 us
    all_to_all x2, waiting for transfers between devices, sent_to_all(): return lax.all_to_all(copies, axis, split_axis=0, concat_axis=0, tiled=True)  14 us
    all_to_all x2, starting transfers between devices, sent_to_all(): return lax.all_to_all(copies, axis, split_axis=0, concat_axis=0, tiled=True)  11 us
    all_to_all x1, waiting for transfers between devices, summed_on_arrival(): tiles = lax.all_to_all(cut_along(value, dim, size), axis, 0, 0, tiled=True)  8.82 us
    dot_general x1, matrix products, local(): jnp.einsum('ebf,edf->bed', pre_grad, weight_in, preferred_element_type=jn...  8.02 us
    unnamed x15, local copies, waits for them, and re-layouts  5.66 us
  transfers between devices with their start and end apart: 4, of which 4 were waited for; matrix products, arithmetic and copies ran while one was open for 6% of the time, Pallas kernels for 0%

commit v1 on v0

v1 whole, which is shorter than its diff:
```python
import functools
import math

import jax
import jax.numpy as jnp
from jax import lax
from jax.experimental import pallas as pl
from jax.experimental.pallas import tpu as pltpu
from jax.sharding import PartitionSpec as P

BF = jnp.bfloat16
F32 = jnp.float32
NX, NZ, NY = 4, 8, 2
NI = NX * NZ * NY
TOK = 196
PAD = 208
D = 1024
S = 128
NT = 512
CH = (3, 0, 2, 1)


def dz_of(k, p):
    if k == 0:
        return 4 * p
    return k if p == 0 else NZ - k


def dot(a, b, ca, cb):
    return lax.dot_general(a, b, (((ca,), (cb,)), ((), ())), preferred_element_type=F32)


def kernel(
    tok, og, router, w_in, w_out,
    tg_out, rg_out,
    win, wout, disp, comb, sbuf, x, fs, lhs, dg, act, pg, s0, s1,
    cbuf, pbuf, ybuf, rbuf, abuf, so, so_m, rgb, rr, tgb, qs,
    wsem, send1, recv1, ysend, yrecv, csend, crecv,
    psend, precv, bsend, brecv, asend, arecv,
    rsend, rrecv, qsend, qrecv, tsend, trecv,
):
    inner = lax.axis_index("inner")
    group = lax.axis_index("group")
    yh = lax.rem(inner, NY)
    zc = lax.rem(lax.div(inner, NY), NZ)
    xc = lax.div(inner, NY * NZ)
    yl = lax.div(group, 2)
    core = lax.rem(group, 2)

    def away(dx, dz, dy):
        x2, z2 = lax.rem(xc + dx, NX), lax.rem(zc + dz, NZ)
        y2, l2 = lax.rem(yh + dy, 2), lax.rem(yl + dy, 2)
        return (x2 * NZ + z2) * NY + y2, l2 * 2 + core

    def target(k, p, t, back):
        dx, dy, dz = lax.rem(t, NX), lax.div(t, NX), dz_of(k, p)
        if back:
            return away(NX - dx, NZ - dz, dy)
        return away(dx, dz, dy)

    def each_peer(fn, chunks=CH):
        for k in chunks:
            if k == 0:
                fn(0, 1, jnp.int32(0))
                lo = 1
            else:
                lo = 0

            @pl.loop(lo, 8)
            def _(t):
                fn(k, 0, t)
                fn(k, 1, t)

    def quad(j):
        return lax.rem(yl + j // 2, 2) * 2 + lax.rem(core + j % 2, 2)

    def dev(g, i):
        return {"group": g, "inner": i}

    barrier = pltpu.get_barrier_semaphore()

    def greet(k, p, t):
        i2, g2 = target(k, p, t, False)
        pl.semaphore_signal(barrier, inc=1, device_id=dev(g2, i2))

    each_peer(greet)
    for j in range(1, 4):
        pl.semaphore_signal(barrier, inc=1, device_id=dev(quad(j), inner))

    wcopy_in = pltpu.make_async_copy(w_in, win, wsem.at[0])
    wcopy_out = pltpu.make_async_copy(w_out, wout, wsem.at[1])
    wcopy_in.start()
    wcopy_out.start()

    logits = dot(tok[...], router[...], 1, 0)
    keep = lax.broadcasted_iota(jnp.int32, (PAD, S), 0) < TOK
    top = jnp.max(jnp.where(keep, logits, -jnp.inf), axis=0, keepdims=True)
    e = jnp.where(keep, jnp.exp(jnp.where(keep, logits - top, 0.0)), 0.0)
    disp[...] = e / jnp.sum(e, axis=0, keepdims=True)
    e = jnp.exp(logits - jnp.max(logits, axis=1, keepdims=True))
    comb[...] = e / jnp.sum(e, axis=1, keepdims=True)

    def to_tiles(kind, weights, values):
        flipped = weights.T.astype(BF)
        val = dot(flipped, values[...], 1, 0)
        for a in range(8):
            fs[pl.ds(a, S, stride=8), :] = val[:, a * 128 : (a + 1) * 128]
        sbuf[kind] = fs[...].reshape(S, 8, 128).astype(BF)

    def send_kind(kind):
        def send(k, p, t):
            i2, g2 = target(k, p, t, False)
            r = k * 16 + t * 2 + p
            pltpu.make_async_remote_copy(
                sbuf.at[kind, pl.ds(i2 * 2, 2)],
                x.at[kind, 0, r],
                send1.at[kind],
                recv1.at[kind, k],
                device_id=dev(g2, i2),
            ).start()

        pltpu.make_async_copy(
            sbuf.at[kind, pl.ds(inner * 2, 2)], x.at[kind, 0, 0], recv1.at[kind, 0]
        ).start()
        each_peer(send)

    to_tiles(0, disp[...], tok)
    pl.semaphore_wait(barrier, NI - 1 + 3)
    send_kind(0)
    to_tiles(1, comb[...], og)
    send_kind(1)

    def part(kind, q, k):
        return x.at[kind, q, pl.ds(k * 16, 16)]

    def ycopy(kind, k):
        return pltpu.make_async_remote_copy(
            part(kind, 0, k), part(kind, 1, k), ysend.at[kind, k], yrecv.at[kind, k],
            device_id=dev(quad(2), inner),
        )

    def ccopy(kind, q, k):
        return pltpu.make_async_remote_copy(
            part(kind, q, k), part(kind, q + 2, k), csend.at[kind, q, k], crecv.at[kind, q, k],
            device_id=dev(quad(1), inner),
        )

    def forward(kind):
        for k in CH:
            pltpu.make_async_copy(part(kind, 0, k), part(kind, 0, k), recv1.at[kind, k]).wait()
            ycopy(kind, k).start()
            ccopy(kind, 0, k).start()
        for k in CH:
            ycopy(kind, k).wait_recv()
            ccopy(kind, 1, k).start()

    def settle(kind):
        for q in range(2):
            for k in CH:
                ccopy(kind, q, k).wait_recv()

    def to_rows(kind, q):
        fs[...] = x[kind, q].astype(F32).reshape(1024, 128)
        for ex in range(2):
            for a in range(8):
                lhs[kind, ex, q * 64 : (q + 1) * 64, a * 128 : (a + 1) * 128] = fs[
                    pl.ds(ex * 8 + a, 64, stride=16), :
                ].astype(BF)

    def scatter_rows(dst, ex, n, val):
        for q in range(4):
            for a in range(NT // 128):
                dst[pl.ds(q * 1024 + ex * 8 + n * (NT // 128) + a, 64, stride=16), :] = val[
                    q * 64 : (q + 1) * 64, a * 128 : (a + 1) * 128
                ]

    c0 = math.sqrt(2.0 / math.pi)

    forward(0)
    to_rows(0, 0)
    to_rows(0, 1)
    settle(0)
    to_rows(0, 2)
    to_rows(0, 3)
    wcopy_in.wait()
    wcopy_out.wait()
    for ex in range(2):
        for n in range(D // NT):
            cols = slice(n * NT, (n + 1) * NT)
            h = dot(lhs[0, ex], win[ex, :, cols], 1, 0)
            h2 = h * h
            th = jnp.tanh(c0 * (h + 0.044715 * h2 * h))
            half = 0.5 * (1.0 + th)
            act[:, cols] = (h * half).astype(BF)
            dg[ex, :, cols] = half + 0.5 * h * (1.0 - th * th) * (
                c0 * (1.0 + (3.0 * 0.044715) * h2)
            )
        for n in range(D // NT):
            scatter_rows(s0, ex, n, dot(act[...], wout[ex, :, n * NT : (n + 1) * NT], 1, 0))

    def pcopy(kind, q):
        return pltpu.make_async_remote_copy(
            cbuf.at[kind, q], pbuf.at[kind, q], psend.at[kind, q], precv.at[kind, q],
            device_id=dev(quad(1), inner),
        )

    def bcopy(kind):
        return pltpu.make_async_remote_copy(
            ybuf.at[kind], rbuf.at[kind], bsend.at[kind], brecv.at[kind],
            device_id=dev(quad(2), inner),
        )

    def quarter(src, q):
        return src[q * 1024 : (q + 1) * 1024, :].reshape(64, 2, 8, 128)

    def reduce_1(kind, src):
        for q in (1, 0):
            cbuf[kind, q] = quarter(src, q + 2).astype(BF)
            pcopy(kind, q).start()

    def reduce_2(kind, src):
        pcopy(kind, 1).wait_recv()
        ybuf[kind] = (quarter(src, 1) + pbuf[kind, 1].astype(F32)).astype(BF)
        bcopy(kind).start()

    def reduce_3(kind, src):
        pcopy(kind, 0).wait_recv()
        bcopy(kind).wait_recv()
        abuf[kind] = (
            quarter(src, 0) + pbuf[kind, 0].astype(F32) + rbuf[kind].astype(F32)
        ).astype(BF)

        def send(k, p, t):
            i2, g2 = target(k, p, t, True)
            r = k * 16 + t * 2 + p
            pltpu.make_async_remote_copy(
                abuf.at[kind, r], so.at[kind, inner], asend.at[kind], arecv.at[kind],
                device_id=dev(g2, i2),
            ).start()

        pltpu.make_async_copy(abuf.at[kind, 0], so.at[kind, inner], arecv.at[kind]).start()
        each_peer(send)

    reduce_1(0, s0)
    forward(1)
    to_rows(1, 0)
    to_rows(1, 1)
    settle(1)
    to_rows(1, 2)
    to_rows(1, 3)
    reduce_2(0, s0)
    for ex in range(2):
        for n in range(D // NT):
            cols = slice(n * NT, (n + 1) * NT)
            ag = dot(lhs[1, ex], wout[ex, cols, :], 1, 1)
            pg[:, cols] = (dg[ex, :, cols] * ag).astype(BF)
        for n in range(D // NT):
            scatter_rows(s1, ex, n, dot(pg[...], win[ex, n * NT : (n + 1) * NT, :], 1, 1))
        if ex == 0:
            reduce_3(0, s0)
    reduce_1(1, s1)
    reduce_2(1, s1)
    reduce_3(1, s1)

    def gather_rows(kind):
        pltpu.make_async_copy(so.at[kind], so.at[kind], arecv.at[kind]).wait()
        fs[...] = so[kind].astype(F32).reshape(1024, 128)
        for a in range(8):
            so_m[kind, :, a * 128 : (a + 1) * 128] = fs[pl.ds(a, S, stride=8), :].astype(BF)

    gather_rows(0)
    cg = dot(og[...], so_m[0], 1, 1)
    cw = comb[...]
    lg = cw * (cg - jnp.sum(cw * cg, axis=1, keepdims=True))
    gather_rows(1)
    dgr = dot(tok[...], so_m[1], 1, 1)
    dw = disp[...]
    lg = lg + dw * (dgr - jnp.sum(dw * dgr, axis=0, keepdims=True))
    lb = lg.astype(BF)
    rgb[...] = dot(tok[...], lb, 0, 0).astype(BF).reshape(NI, 16, 128)

    def send_router(k, p, t):
        i2, g2 = target(k, p, t, False)
        r = k * 16 + t * 2 + p
        pltpu.make_async_remote_copy(
            rgb.at[i2], rr.at[r], rsend, rrecv, device_id=dev(g2, i2)
        ).start()

    pltpu.make_async_copy(rgb.at[inner], rr.at[0], rrecv).start()
    each_peer(send_router)

    tg = dot(dw.astype(BF), so_m[1], 1, 0) + dot(lb, router[...], 1, 1)
    for g in range(4):
        tgb[g] = tg[:, g * 256 : (g + 1) * 256].astype(BF)

    def tcopy(j):
        g2 = quad(j)
        return pltpu.make_async_remote_copy(
            tgb.at[g2], tg_out.at[group], tsend.at[j], trecv.at[j], device_id=dev(g2, inner)
        )

    for j in (2, 3, 1):
        tcopy(j).start()
    mine = pltpu.make_async_copy(tgb.at[group], tg_out.at[group], tsend.at[0])
    mine.start()

    pltpu.make_async_copy(rr, rr, rrecv).wait()
    qs[0] = jnp.sum(rr[...].astype(F32), axis=0)

    def qcopy(j):
        return pltpu.make_async_remote_copy(
            qs.at[0], qs.at[j], qsend.at[j], qrecv.at[j], device_id=dev(quad(j), inner)
        )

    for j in (2, 3, 1):
        qcopy(j).start()
    for j in range(1, 4):
        tcopy(j).wait()
    mine.wait()
    for j in range(1, 4):
        qcopy(j).wait()
    rg_out[...] = (qs[0] + qs[1]) + (qs[2] + qs[3])

    for kind in range(2):
        pltpu.make_async_copy(
            x.at[kind, 0, pl.ds(1, NI - 1)], x.at[kind, 0, pl.ds(1, NI - 1)], send1.at[kind]
        ).wait()
        pltpu.make_async_copy(
            so.at[kind, pl.ds(1, NI - 1)], so.at[kind, pl.ds(1, NI - 1)], asend.at[kind]
        ).wait()
        for k in CH:
            ycopy(kind, k).wait_send()
            for q in range(2):
                ccopy(kind, q, k).wait_send()
        for q in range(2):
            pcopy(kind, q).wait_send()
        bcopy(kind).wait_send()
    pltpu.make_async_copy(rr.at[pl.ds(1, NI - 1)], rr.at[pl.ds(1, NI - 1)], rsend).wait()


def local(tokens, output_grad, router, weight_in, weight_out):
    g = lax.axis_index("group")

    def mine(a):
        one = lax.dynamic_index_in_dim(a, g, 0, keepdims=False)
        return jnp.pad(one, ((0, PAD - TOK), (0, 0)))

    dma = pltpu.SemaphoreType.DMA
    vm = pl.BlockSpec(memory_space=pltpu.VMEM)
    hbm = pl.BlockSpec(memory_space=pl.ANY)
    tg, rg = pl.pallas_call(
        kernel,
        name="moe_backward",
        out_shape=(
            jax.ShapeDtypeStruct((4, PAD, 256), BF),
            jax.ShapeDtypeStruct((16, S), F32),
        ),
        in_specs=[vm, vm, vm, hbm, hbm],
        out_specs=(vm, vm),
        scratch_shapes=[
            pltpu.VMEM((2, D, D), BF),
            pltpu.VMEM((2, D, D), BF),
            pltpu.VMEM((PAD, S), F32),
            pltpu.VMEM((PAD, S), F32),
            pltpu.VMEM((2, S, 8, 128), BF),
            pltpu.VMEM((2, 4, NI, 2, 8, 128), BF),
            pltpu.VMEM((1024, 128), F32),
            pltpu.VMEM((2, 2, 256, D), BF),
            pltpu.VMEM((2, 256, D), F32),
            pltpu.VMEM((256, D), BF),
            pltpu.VMEM((256, D), BF),
            pltpu.VMEM((4096, 128), F32),
            pltpu.VMEM((4096, 128), F32),
            pltpu.VMEM((2, 2, NI, 2, 8, 128), BF),
            pltpu.VMEM((2, 2, NI, 2, 8, 128), BF),
            pltpu.VMEM((2, NI, 2, 8, 128), BF),
            pltpu.VMEM((2, NI, 2, 8, 128), BF),
            pltpu.VMEM((2, NI, 2, 8, 128), BF),
            pltpu.VMEM((2, NI, 2, 8, 128), BF),
            pltpu.VMEM((2, S, D), BF),
            pltpu.VMEM((NI, 16, 128), BF),
            pltpu.VMEM((NI, 16, 128), BF),
            pltpu.VMEM((4, PAD, 256), BF),
            pltpu.VMEM((4, 16, 128), F32),
            dma((2,)),
            dma((2,)), dma((2, 4)),
            dma((2, 4)), dma((2, 4)),
            dma((2, 2, 4)), dma((2, 2, 4)),
            dma((2, 2)), dma((2, 2)),
            dma((2,)), dma((2,)),
            dma((2,)), dma((2,)),
            dma, dma,
            dma((4,)), dma((4,)),
            dma((4,)), dma((4,)),
        ],
        compiler_params=pltpu.CompilerParams(
            collective_id=0, has_side_effects=True, vmem_limit_bytes=58 * 1024 * 1024
        ),
    )(mine(tokens), mine(output_grad), router, weight_in, weight_out)
    return tg[:, :TOK], rg


def solution(mesh):
    return jax.shard_map(
        local,
        mesh=mesh,
        in_specs=(
            P("inner", None, None),
            P("inner", None, None),
            P(),
            P("inner", None, "group"),
            P("inner", "group", None),
        ),
        out_specs=(P("inner", None, "group"), P("inner", None)),
        check_vma=False,
    )
```

time: 217 us -> 94.2 us (0.43)
  blocking collectives: 95.9 us -> 0 us
  Pallas kernels: 0 us -> 84.6 us
  waiting for transfers between devices: 37.9 us -> 0 us
  matrix products: 31.5 us -> 0 us
  starting transfers between devices: 22.3 us -> 0 us
  other arithmetic: 10.5 us -> 0 us
  local copies, waits for them, and re-layouts: 15.8 us -> 7.97 us
    all_to_all x2 -> x0, blocking collectives: 95.9 us -> none  [the longest x1 66.1 us: in_one_piece(): lax.all_to_all(both, axis, split_axis=split_dim, concat_axis=concat_dim,...]
    pallas_call x0 -> x1, Pallas kernels: none -> 84.6 us  [local(): pl.pallas_call(kernel, name='moe_backward', out_shape=(jax.ShapeDtypeStru...]
    all_to_all x4 -> x0, waiting for transfers between devices: 37.9 us -> none  [the longest x1 15.1 us: in_one_piece(): lax.all_to_all(both, axis, split_axis=split_dim, concat_axis=concat_dim,...]
    dot_general x11 -> x0, matrix products: 31.5 us -> none  [the longest x1 8.02 us: local(): jnp.einsum('ebf,edf->bed', pre_grad, weight_in, preferred_element_type=jn...]
    all_to_all x4 -> x0, starting transfers between devices: 22.3 us -> none  [the longest x2 11 us: sent_to_all(): return lax.all_to_all(copies, axis, split_axis=0, concat_axis=0, tiled=True)]
    sub x3 -> x0, other arithmetic: 6.83 us -> none  [the longest x1 5.03 us: local(): combine_grad - jnp.sum(combine * combine_grad, axis=2, keepdims=True)]
    unnamed x15 -> x6, local copies, waits for them, and re-layouts: 5.66 us -> 1.76 us
    all_to_all x4 -> x0, local copies, waits for them, and re-layouts: 3.8 us -> none  [in_one_piece(): lax.all_to_all(both, axis, split_axis=split_dim, concat_axis=concat_dim,...]
  transfers between devices with their start and end apart: 4 -> 0, of which waited for: 4 -> 0; matrix products, arithmetic and copies ran while one was open for 6% -> 0% of each run, Pallas kernels for 0% -> 0%
where the time goes in v1:
time: 94.2 us; the launch traced here: 93.2 us
  Pallas kernels  84.6 us (90%)
  local copies, waits for them, and re-layouts  7.97 us (8%)
    pallas_call x1, Pallas kernels, local(): pl.pallas_call(kernel, name='moe_backward', out_shape=(jax.ShapeDtypeStru...  84.6 us
    dynamic_slice x1, local copies, waits for them, and re-layouts, mine(): one = lax.dynamic_index_in_dim(a, g, 0, keepdims=False)  3.56 us

profile of v1, /device:TPU:1, one launch (start us, length us, event | category | flops | bytes accessed | tf_op | source)
XLA Modules:
  0.0 93.2 jit_solution(13163759972323240439)
XLA Ops:
  0.6 3.6 %constant_dynamic-slice_fusion = (bf16[1,196,1024]{2,0,1:T(2,128)(2,1)S(1)}, bf16[1,196,1024]{2,0,1:T(2,128)(2,1)S(1)}) fusion(bf16[4,196,1024]{2,0,1:T(4,128)(2,1)} %param.6, s32[]{:T(128)S(6)} %select_n.5, bf16[4,196,1024]{2,0,1:T(4,128)(2,1)} %param.5), kind=kLoop, calls=%fused_computation.2 | loop fusion | bytes 1605636 | tf_op jit(solution)/shard_map/jit(dynamic_index_in_dim)/dynamic_slice | solution.py:345
  4.2 0.1 copy.15
  4.3 0.8 pad.8.og
  5.2 0.1 copy.16
  5.3 0.8 pad.7.tok
  6.1 84.6 %moe_backward.1 = (bf16[4,208,256]{2,1,0:T(8,128)(2,1)}, f32[16,128]{1,0:T(8,128)}) custom-call(bf16[208,1024]{1,0:T(8,128)(2,1)} %pad.7.tok, bf16[208,1024]{1,0:T(8,128)(2,1)} %pad.8.og, bf16[1024,128]{1,0:T(8,128)(2,1)} %router.1, bf16[2,1024,1024]{2,1,0:T(8,128)(2,1)} %w_in.1, bf16[2,1024,1024]{2,1,0:T(8,128)(2,1)} %w_out.1), custom_call_target="tpu_custom_call" | custom-call | tf_op jit(solution)/shard_map/moe_backward/pallas_call | solution.py:351
  90.6 0.0 copy-start
  90.7 1.0 %slice.3 = bf16[4,196,256]{2,1,0:T(8,128)(2,1)S(1)} slice(bf16[4,208,256]{2,1,0:T(8,128)(2,1)} %get-tuple-element.4), slice={[0:4], [0:196], [0:256]} | slice | bytes 802816 | tf_op jit(solution)/shard_map/slice | solution.py:400
  91.7 0.9 copy.10
  92.6 0.0 copy-done
  92.6 0.6 copy.18
Async XLA Ops:
  90.6 2.0 %copy-start = (f32[16,128]{1,0:T(8,128)S(1)}, f32[16,128]{1,0:T(8,128)}, u32[]{:S(2)}) copy-start(f32[16,128]{1,0:T(8,128)} %get-tuple-element.15) | copy-start | bytes 24580

commit v2 on v1

--- a/solution.py
+++ b/solution.py
@@ -1,4 +1,4 @@
-import functools
+import contextlib
 import math
 
 import jax
@@ -16,8 +16,13 @@
 PAD = 208
 D = 1024
 S = 128
+RAW = TOK * 32
 NT = 512
 CH = (3, 0, 2, 1)
+
+
+def scope(name):
+    return contextlib.nullcontext()
 
 
 def dz_of(k, p):
@@ -31,13 +36,13 @@
 
 
 def kernel(
-    tok, og, router, w_in, w_out,
+    tok_all, og_all, router, w_in, w_out,
     tg_out, rg_out,
-    win, wout, disp, comb, sbuf, x, fs, lhs, dg, act, pg, s0, s1,
-    cbuf, pbuf, ybuf, rbuf, abuf, so, so_m, rgb, rr, tgb, qs,
-    wsem, send1, recv1, ysend, yrecv, csend, crecv,
+    raw, wide, tok, og, land, win, wout, disp, comb, sbuf, x, fs, lhs, dg, act, pg, s0, s1,
+    cbuf, pbuf, ybuf, rbuf, abuf, so, so_m, rgo, rgs, rgp, rgb, rr, tgb, qs,
+    tsem, wsem, send1, recv1, ysend, yrecv, csend, crecv,
     psend, precv, bsend, brecv, asend, arecv,
-    rsend, rrecv, qsend, qrecv, tsend, trecv,
+    gsend, grecv, rsend, rrecv, qsend, qrecv, tsend, trecv,
 ):
     inner = lax.axis_index("inner")
     group = lax.axis_index("group")
@@ -87,11 +92,33 @@
     for j in range(1, 4):
         pl.semaphore_signal(barrier, inc=1, device_id=dev(quad(j), inner))
 
+    def fetch(kind, n):
+        src = (tok_all, og_all)[kind]
+        rows = pl.ds(n * (RAW // 4), RAW // 4)
+        return pltpu.make_async_copy(src.at[rows], raw.at[kind, rows], tsem.at[kind, n])
+
+    for kind in range(2):
+        for n in range(4):
+            fetch(kind, n).start()
     wcopy_in = pltpu.make_async_copy(w_in, win, wsem.at[0])
     wcopy_out = pltpu.make_async_copy(w_out, wout, wsem.at[1])
     wcopy_in.start()
     wcopy_out.start()
 
+    wide[RAW:, :] = jnp.zeros((PAD * 32 - RAW, 128), F32)
+
+    def extract(kind, dst):
+        for n in range(4):
+            fetch(kind, n).wait()
+            rows = slice(n * (RAW // 4), (n + 1) * (RAW // 4))
+            wide[rows, :] = raw[kind, rows, :].astype(F32)
+        for a in range(8):
+            dst[:, a * 128 : (a + 1) * 128] = wide[
+                pl.ds(a * 4 + group, PAD, stride=32), :
+            ].astype(BF)
+
+    with scope("extract0"):
+        extract(0, tok)
     logits = dot(tok[...], router[...], 1, 0)
     keep = lax.broadcasted_iota(jnp.int32, (PAD, S), 0) < TOK
     top = jnp.max(jnp.where(keep, logits, -jnp.inf), axis=0, keepdims=True)
@@ -124,11 +151,18 @@
         ).start()
         each_peer(send)
 
-    to_tiles(0, disp[...], tok)
-    pl.semaphore_wait(barrier, NI - 1 + 3)
-    send_kind(0)
-    to_tiles(1, comb[...], og)
-    send_kind(1)
+    with scope("tiles0"):
+        to_tiles(0, disp[...], tok)
+    with scope("barrier"):
+        pl.semaphore_wait(barrier, NI - 1 + 3)
+    with scope("send0"):
+        send_kind(0)
+    with scope("extract1"):
+        extract(1, og)
+    with scope("tiles1"):
+        to_tiles(1, comb[...], og)
+    with scope("send1"):
+        send_kind(1)
 
     def part(kind, q, k):
         return x.at[kind, q, pl.ds(k * 16, 16)]
@@ -145,14 +179,14 @@
             device_id=dev(quad(1), inner),
         )
 
-    def forward(kind):
-        for k in CH:
-            pltpu.make_async_copy(part(kind, 0, k), part(kind, 0, k), recv1.at[kind, k]).wait()
-            ycopy(kind, k).start()
-            ccopy(kind, 0, k).start()
-        for k in CH:
-            ycopy(kind, k).wait_recv()
-            ccopy(kind, 1, k).start()
+    def forward_a(kind, k):
+        pltpu.make_async_copy(part(kind, 0, k), part(kind, 0, k), recv1.at[kind, k]).wait()
+        ycopy(kind, k).start()
+        ccopy(kind, 0, k).start()
+
+    def forward_b(kind, k):
+        ycopy(kind, k).wait_recv()
+        ccopy(kind, 1, k).start()
 
     def settle(kind):
         for q in range(2):
@@ -176,15 +210,56 @@
 
     c0 = math.sqrt(2.0 / math.pi)
 
-    forward(0)
-    to_rows(0, 0)
-    to_rows(0, 1)
-    settle(0)
-    to_rows(0, 2)
-    to_rows(0, 3)
-    wcopy_in.wait()
-    wcopy_out.wait()
-    for ex in range(2):
+    def pcopy(kind, q):
+        return pltpu.make_async_remote_copy(
+            cbuf.at[kind, q], pbuf.at[kind, q], psend.at[kind, q], precv.at[kind, q],
+            device_id=dev(quad(1), inner),
+        )
+
+    def bcopy(kind, k):
+        sel = pl.ds(k * 16, 16)
+        return pltpu.make_async_remote_copy(
+            ybuf.at[kind, sel], rbuf.at[kind, sel], bsend.at[kind, k], brecv.at[kind, k],
+            device_id=dev(quad(2), inner),
+        )
+
+    def quarter(src, q):
+        return src[q * 1024 : (q + 1) * 1024, :].reshape(64, 2, 8, 128)
+
+    def reduce_1(kind, src):
+        for q in (1, 0):
+            cbuf[kind, q] = quarter(src, q + 2).astype(BF)
+            pcopy(kind, q).start()
+
+    def chunk(src, q, k):
+        return src[q * 1024 + k * 256 : q * 1024 + (k + 1) * 256, :].reshape(16, 2, 8, 128)
+
+    def reduce_2(kind, src):
+        pcopy(kind, 1).wait_recv()
+        for k in CH:
+            sel = pl.ds(k * 16, 16)
+            ybuf[kind, sel] = (chunk(src, 1, k) + pbuf[kind, 1, sel].astype(F32)).astype(BF)
+            bcopy(kind, k).start()
+        pcopy(kind, 0).wait_recv()
+        src[0:1024, :] = src[0:1024, :] + pbuf[kind, 0].astype(F32).reshape(1024, 128)
+
+    def reduce_3(kind, src, k):
+        sel = pl.ds(k * 16, 16)
+        bcopy(kind, k).wait_recv()
+        abuf[kind, sel] = (chunk(src, 0, k) + rbuf[kind, sel].astype(F32)).astype(BF)
+        if k == 0:
+            pltpu.make_async_copy(abuf.at[kind, 0], so.at[kind, inner], arecv.at[kind]).start()
+
+        def send(k, p, t):
+            i2, g2 = target(k, p, t, True)
+            pltpu.make_async_remote_copy(
+                abuf.at[kind, k * 16 + t * 2 + p], so.at[kind, inner], asend.at[kind],
+                arecv.at[kind], device_id=dev(g2, i2),
+            ).start()
+
+        each_peer(send, (k,))
+
+    def pre(ex):
         for n in range(D // NT):
             cols = slice(n * NT, (n + 1) * NT)
             h = dot(lhs[0, ex], win[ex, :, cols], 1, 0)
@@ -195,72 +270,87 @@
             dg[ex, :, cols] = half + 0.5 * h * (1.0 - th * th) * (
                 c0 * (1.0 + (3.0 * 0.044715) * h2)
             )
+
+    def out(ex):
         for n in range(D // NT):
             scatter_rows(s0, ex, n, dot(act[...], wout[ex, :, n * NT : (n + 1) * NT], 1, 0))
 
-    def pcopy(kind, q):
-        return pltpu.make_async_remote_copy(
-            cbuf.at[kind, q], pbuf.at[kind, q], psend.at[kind, q], precv.at[kind, q],
-            device_id=dev(quad(1), inner),
-        )
-
-    def bcopy(kind):
-        return pltpu.make_async_remote_copy(
-            ybuf.at[kind], rbuf.at[kind], bsend.at[kind], brecv.at[kind],
-            device_id=dev(quad(2), inner),
-        )
-
-    def quarter(src, q):
-        return src[q * 1024 : (q + 1) * 1024, :].reshape(64, 2, 8, 128)
-
-    def reduce_1(kind, src):
-        for q in (1, 0):
-            cbuf[kind, q] = quarter(src, q + 2).astype(BF)
-            pcopy(kind, q).start()
-
-    def reduce_2(kind, src):
-        pcopy(kind, 1).wait_recv()
-        ybuf[kind] = (quarter(src, 1) + pbuf[kind, 1].astype(F32)).astype(BF)
-        bcopy(kind).start()
-
-    def reduce_3(kind, src):
-        pcopy(kind, 0).wait_recv()
-        bcopy(kind).wait_recv()
-        abuf[kind] = (
-            quarter(src, 0) + pbuf[kind, 0].astype(F32) + rbuf[kind].astype(F32)
-        ).astype(BF)
-
-        def send(k, p, t):
-            i2, g2 = target(k, p, t, True)
-            r = k * 16 + t * 2 + p
-            pltpu.make_async_remote_copy(
-                abuf.at[kind, r], so.at[kind, inner], asend.at[kind], arecv.at[kind],
-                device_id=dev(g2, i2),
-            ).start()
-
-        pltpu.make_async_copy(abuf.at[kind, 0], so.at[kind, inner], arecv.at[kind]).start()
-        each_peer(send)
-
-    reduce_1(0, s0)
-    forward(1)
-    to_rows(1, 0)
-    to_rows(1, 1)
-    settle(1)
-    to_rows(1, 2)
-    to_rows(1, 3)
-    reduce_2(0, s0)
-    for ex in range(2):
+    def act_grad(ex):
         for n in range(D // NT):
             cols = slice(n * NT, (n + 1) * NT)
             ag = dot(lhs[1, ex], wout[ex, cols, :], 1, 1)
             pg[:, cols] = (dg[ex, :, cols] * ag).astype(BF)
+
+    def back(ex):
         for n in range(D // NT):
             scatter_rows(s1, ex, n, dot(pg[...], win[ex, n * NT : (n + 1) * NT, :], 1, 1))
-        if ex == 0:
-            reduce_3(0, s0)
-    reduce_1(1, s1)
-    reduce_2(1, s1)
-    reduce_3(1, s1)
+
+    with scope("fwdA0"):
+        for k in CH:
+            forward_a(0, k)
+    with scope("fwdA1_0"):
+        forward_a(1, CH[0])
+    with scope("fwdB0"):
+        for k in CH:
+            forward_b(0, k)
+    with scope("rows0ab"):
+        to_rows(0, 0)
+        to_rows(0, 1)
+    with scope("settle0"):
+        settle(0)
+    with scope("rows0cd"):
+        to_rows(0, 2)
+        to_rows(0, 3)
+    with scope("fwdA1_1"):
+        forward_a(1, CH[1])
+    wcopy_in.wait()
+    wcopy_out.wait()
+    with scope("pre"):
+        pre(0)
+    with scope("fwdA1_2"):
+        forward_a(1, CH[2])
+    with scope("out"):
+        out(0)
+    with scope("fwdA1_3"):
+        forward_a(1, CH[3])
+    with scope("pre"):
+        pre(1)
+    with scope("fwdB1"):
+        forward_b(1, CH[0])
+    with scope("out"):
+        out(1)
+    with scope("reduce1_0"):
+        reduce_1(0, s0)
+    with scope("fwdB1"):
+        for k in CH[1:]:
+            forward_b(1, k)
+    with scope("reduce2_0"):
+        reduce_2(0, s0)
+    with scope("rows1ab"):
+        to_rows(1, 0)
+        to_rows(1, 1)
+    with scope("settle1"):
+        settle(1)
+    with scope("rows1cd"):
+        to_rows(1, 2)
+        to_rows(1, 3)
+    for ex in range(2):
+        with scope("actgrad"):
+            act_grad(ex)
+        with scope("back"):
+            back(ex)
+    with scope("reduce1_1"):
+        reduce_1(1, s1)
+    with scope("reduce3_0"):
+        reduce_3(0, s0, CH[0])
+    with scope("reduce2_1"):
+        reduce_2(1, s1)
+    for k in CH[1:]:
+        with scope("reduce3_0"):
+            reduce_3(0, s0, k)
+    for k in CH:
+        with scope("reduce3_1"):
+            reduce_3(1, s1, k)
 
     def gather_rows(kind):
         pltpu.make_async_copy(so.at[kind], so.at[kind], arecv.at[kind]).wait()
@@ -268,43 +358,69 @@
         for a in range(8):
             so_m[kind, :, a * 128 : (a + 1) * 128] = fs[pl.ds(a, S, stride=8), :].astype(BF)
 
-    gather_rows(0)
+    with scope("gather0"):
+        gather_rows(0)
     cg = dot(og[...], so_m[0], 1, 1)
     cw = comb[...]
     lg = cw * (cg - jnp.sum(cw * cg, axis=1, keepdims=True))
-    gather_rows(1)
+    with scope("gather1"):
+        gather_rows(1)
     dgr = dot(tok[...], so_m[1], 1, 1)
     dw = disp[...]
     lg = lg + dw * (dgr - jnp.sum(dw * dgr, axis=0, keepdims=True))
     lb = lg.astype(BF)
-    rgb[...] = dot(tok[...], lb, 0, 0).astype(BF).reshape(NI, 16, 128)
-
-    def send_router(k, p, t):
-        i2, g2 = target(k, p, t, False)
-        r = k * 16 + t * 2 + p
-        pltpu.make_async_remote_copy(
-            rgb.at[i2], rr.at[r], rsend, rrecv, device_id=dev(g2, i2)
-        ).start()
-
-    pltpu.make_async_copy(rgb.at[inner], rr.at[0], rrecv).start()
-    each_peer(send_router)
-
-    tg = dot(dw.astype(BF), so_m[1], 1, 0) + dot(lb, router[...], 1, 1)
-    for g in range(4):
-        tgb[g] = tg[:, g * 256 : (g + 1) * 256].astype(BF)
+    rg = dot(tok[...], lb, 0, 0).reshape(NI, 2, 8, 128)
+    rgo[...] = rg
+    rgs[...] = rgo[:, pl.ds(1 - core, 1)].reshape(NI, 8, 128).astype(BF)
+
+    gcopy = pltpu.make_async_remote_copy(
+        rgs, rgp, gsend, grecv, device_id=dev(quad(1), inner)
+    )
+    gcopy.start()
+    with scope("tg"):
+        tg = dot(dw.astype(BF), so_m[1], 1, 0) + dot(lb, router[...], 1, 1)
+        for g in range(4):
+            tgb[g] = tg[:, g * 256 : (g + 1) * 256].astype(BF)
 
     def tcopy(j):
         g2 = quad(j)
         return pltpu.make_async_remote_copy(
-            tgb.at[g2], tg_out.at[group], tsend.at[j], trecv.at[j], device_id=dev(g2, inner)
+            tgb.at[g2], land.at[group], tsend.at[j], trecv.at[j], device_id=dev(g2, inner)
         )
 
+    gcopy.wait_recv()
+    rgb[...] = (
+        rgo[:, pl.ds(core, 1)].reshape(NI, 8, 128) + rgp[...].astype(F32)
+    ).astype(BF)
+
+    def send_router(k, p, t):
+        i2, g2 = target(k, p, t, False)
+        pltpu.make_async_remote_copy(
+            rgb.at[i2], rr.at[k * 16 + t * 2 + p], rsend, rrecv, device_id=dev(g2, i2)
+        ).start()
+
+    with scope("send_router"):
+        pltpu.make_async_copy(rgb.at[inner], rr.at[0], rrecv).start()
+        each_peer(send_router)
     for j in (2, 3, 1):
         tcopy(j).start()
-    mine = pltpu.make_async_copy(tgb.at[group], tg_out.at[group], tsend.at[0])
+    mine = pltpu.make_async_copy(tgb.at[group], land.at[group], tsend.at[0])
     mine.start()
 
-    pltpu.make_async_copy(rr, rr, rrecv).wait()
+    with scope("wait_tg"):
+        for j in range(1, 4):
+            tcopy(j).wait()
+        mine.wait()
+    with scope("tg_out"):
+        for g in range(4):
+            for a in range(2):
+                wide[pl.ds(a * 4 + g, PAD, stride=8), :] = land[
+                    g, :, a * 128 : (a + 1) * 128
+                ].astype(F32)
+        tg_out[...] = wide[: TOK * 8, :].astype(BF)
+
+    with scope("wait_router"):
+        pltpu.make_async_copy(rr, rr, rrecv).wait()
     qs[0] = jnp.sum(rr[...].astype(F32), axis=0)
 
     def qcopy(j):
@@ -314,12 +430,11 @@
 
     for j in (2, 3, 1):
         qcopy(j).start()
-    for j in range(1, 4):
-        tcopy(j).wait()
-    mine.wait()
-    for j in range(1, 4):
-        qcopy(j).wait()
-    rg_out[...] = (qs[0] + qs[1]) + (qs[2] + qs[3])
+    with scope("wait_q"):
+        for j in range(1, 4):
+            qcopy(j).wait()
+    rg_out[pl.ds(core * 8, 8), :] = qs[0] + qs[2]
+    rg_out[pl.ds((1 - core) * 8, 8), :] = qs[1] + qs[3]
 
     for kind in range(2):
         pltpu.make_async_copy(
@@ -334,16 +449,16 @@
                 ccopy(kind, q, k).wait_send()
         for q in range(2):
             pcopy(kind, q).wait_send()
-        bcopy(kind).wait_send()
+        for k in CH:
+            bcopy(kind, k).wait_send()
+    gcopy.wait_send()
     pltpu.make_async_copy(rr.at[pl.ds(1, NI - 1)], rr.at[pl.ds(1, NI - 1)], rsend).wait()
 
 
 def local(tokens, output_grad, router, weight_in, weight_out):
-    g = lax.axis_index("group")
-
-    def mine(a):
-        one = lax.dynamic_index_in_dim(a, g, 0, keepdims=False)
-        return jnp.pad(one, ((0, PAD - TOK), (0, 0)))
+    def as_stored(a):
+        a = a.transpose(1, 0, 2).reshape(TOK, 4, 8, 128).transpose(0, 2, 1, 3)
+        return a.reshape(RAW, 128)
 
     dma = pltpu.SemaphoreType.DMA
     vm = pl.BlockSpec(memory_space=pltpu.VMEM)
@@ -352,12 +467,17 @@
         kernel,
         name="moe_backward",
         out_shape=(
-            jax.ShapeDtypeStruct((4, PAD, 256), BF),
+            jax.ShapeDtypeStruct((TOK * 8, 128), BF),
             jax.ShapeDtypeStruct((16, S), F32),
         ),
-        in_specs=[vm, vm, vm, hbm, hbm],
+        in_specs=[hbm, hbm, vm, hbm, hbm],
         out_specs=(vm, vm),
         scratch_shapes=[
+            pltpu.VMEM((2, RAW, 128), BF),
+            pltpu.VMEM((PAD * 32, 128), F32),
+            pltpu.VMEM((PAD, D), BF),
+            pltpu.VMEM((PAD, D), BF),
+            pltpu.VMEM((4, PAD, 256), BF),
             pltpu.VMEM((2, D, D), BF),
             pltpu.VMEM((2, D, D), BF),
             pltpu.VMEM((PAD, S), F32),
@@ -378,17 +498,22 @@
             pltpu.VMEM((2, NI, 2, 8, 128), BF),
             pltpu.VMEM((2, NI, 2, 8, 128), BF),
             pltpu.VMEM((2, S, D), BF),
-            pltpu.VMEM((NI, 16, 128), BF),
-            pltpu.VMEM((NI, 16, 128), BF),
+            pltpu.VMEM((NI, 2, 8, 128), F32),
+            pltpu.VMEM((NI, 8, 128), BF),
+            pltpu.VMEM((NI, 8, 128), BF),
+            pltpu.VMEM((NI, 8, 128), BF),
+            pltpu.VMEM((NI, 8, 128), BF),
             pltpu.VMEM((4, PAD, 256), BF),
-            pltpu.VMEM((4, 16, 128), F32),
+            pltpu.VMEM((4, 8, 128), F32),
+            dma((2, 4)),
             dma((2,)),
             dma((2,)), dma((2, 4)),
             dma((2, 4)), dma((2, 4)),
             dma((2, 2, 4)), dma((2, 2, 4)),
             dma((2, 2)), dma((2, 2)),
+            dma((2, 4)), dma((2, 4)),
             dma((2,)), dma((2,)),
-            dma((2,)), dma((2,)),
+            dma, dma,
             dma, dma,
             dma((4,)), dma((4,)),
             dma((4,)), dma((4,)),
@@ -396,8 +521,9 @@
         compiler_params=pltpu.CompilerParams(
             collective_id=0, has_side_effects=True, vmem_limit_bytes=58 * 1024 * 1024
         ),
-    )(mine(tokens), mine(output_grad), router, weight_in, weight_out)
-    return tg[:, :TOK], rg
+    )(as_stored(tokens), as_stored(output_grad), router, weight_in, weight_out)
+    tg = tg.reshape(TOK, 2, 4, 128).transpose(2, 0, 1, 3).reshape(4, TOK, 256)
+    return tg, rg
 
 
 def solution(mesh):

time: 94.2 us -> 76.2 us (0.81)
  Pallas kernels: 84.6 us -> 72.1 us
  local copies, waits for them, and re-layouts: 7.97 us -> 3.18 us
    pallas_call x1, Pallas kernels: 84.6 us -> 72.1 us  [local(): pl.pallas_call(kernel, name='moe_backward', out_shape=(jax.ShapeDtypeStru...]
    dynamic_slice x1 -> x0, local copies, waits for them, and re-layouts: 3.56 us -> none  [mine(): one = lax.dynamic_index_in_dim(a, g, 0, keepdims=False)]
    pad x2 -> x0, local copies, waits for them, and re-layouts: 1.61 us -> none  [mine(): return jnp.pad(one, ((0, PAD - TOK), (0, 0)))]
    unnamed x6 -> x2, local copies, waits for them, and re-layouts: 1.76 us -> 3.18 us
    slice x1 -> x0, local copies, waits for them, and re-layouts: 1.04 us -> none  [local(): return (tg[:, :TOK], rg)]
where the time goes in v2:
time: 76.2 us; the launch traced here: 76 us
  Pallas kernels  72.1 us (95%)
  local copies, waits for them, and re-layouts  3.18 us (4%)
    pallas_call x1, Pallas kernels, local(): pl.pallas_call(kernel, name='moe_backward', out_shape=(jax.ShapeDtypeStru...  72.1 us
    unnamed x2, local copies, waits for them, and re-layouts  3.18 us

profile of v2, /device:TPU:1, one launch (start us, length us, event | category | flops | bytes accessed | tf_op | source)
XLA Modules:
  0.0 76.0 jit_solution(10215933253208532449)
XLA Ops:
  0.6 72.1 %moe_backward.1 = (bf16[1568,128]{1,0:T(8,128)(2,1)}, f32[16,128]{1,0:T(8,128)}) custom-call(bf16[6272,128]{1,0:T(8,128)(2,1)} %bitcast.19, bf16[6272,128]{1,0:T(8,128)(2,1)} %bitcast.20, bf16[1024,128]{1,0:T(8,128)(2,1)} %router.1, bf16[2,1024,1024]{2,1,0:T(8,128)(2,1)} %w_in.1, bf16[2,1024,1024]{2,1,0:T(8,128)(2,1)} %w_out.1), custom_call_target="tpu_custom_call" | custom-call | tf_op jit(solution)/shard_map/moe_backward/pallas_call | solution.py:466
  72.8 1.9 %copy.12 = bf16[4,196,256]{2,0,1:T(4,128)(2,1)} copy(bf16[4,196,256]{2,0,1:T(4,128)(2,1)} %bitcast.21) | data formatting | bytes 802816
  74.7 1.3 %copy.13 = f32[16,128]{1,0:T(8,128)} copy(f32[16,128]{1,0:T(8,128)} %get-tuple-element.9) | data formatting | bytes 16384

commit v3 on v2

v3 whole, which is shorter than its diff:
```python
import contextlib
import math

import jax
import jax.numpy as jnp
from jax import lax
from jax.experimental import pallas as pl
from jax.experimental.pallas import tpu as pltpu
from jax.sharding import PartitionSpec as P

BF = jnp.bfloat16
F32 = jnp.float32
NX, NZ, NY = 4, 8, 2
NI = NX * NZ * NY
TOK = 196
PAD = 208
D = 1024
S = 128
RAW = TOK * 32
NT = 512
CH = (3, 0, 2, 1)
HALVES = ((3, 0), (2, 1))
SELF = 16


def scope(name):
    return contextlib.nullcontext()


def slot_of(k, p, t):
    return CH.index(k) * 16 + t * 2 + p


def dz_of(k, p):
    if k == 0:
        return 4 * p
    return k if p == 0 else NZ - k


def dot(a, b, ca, cb):
    return lax.dot_general(a, b, (((ca,), (cb,)), ((), ())), preferred_element_type=F32)


def kernel(
    tok_all, og_all, router_all, w_in, w_out,
    land, rg,
    raw, wide, tok, og, router, win, wout, disp, comb, sbuf, x, fs, lhs, dg, act, pg, s0, s1, s2, s3,
    cbuf, pbuf, ybuf, rbuf, abuf, so, so_m, rgo, rgs, rgp, rgb, rr, tgb, qs,
    tsem, wsem, send1, recv1, ysend, yrecv, csend, crecv,
    psend, precv, bsend, brecv, asend, arecv,
    gsend, grecv, rsend, rrecv, qsend, qrecv, tsend, trecv,
):
    inner = lax.axis_index("inner")
    group = lax.axis_index("group")
    yh = lax.rem(inner, NY)
    zc = lax.rem(lax.div(inner, NY), NZ)
    xc = lax.div(inner, NY * NZ)
    yl = lax.div(group, 2)
    core = lax.rem(group, 2)

    def away(dx, dz, dy):
        x2, z2 = lax.rem(xc + dx, NX), lax.rem(zc + dz, NZ)
        y2, l2 = lax.rem(yh + dy, 2), lax.rem(yl + dy, 2)
        return (x2 * NZ + z2) * NY + y2, l2 * 2 + core

    def target(k, p, t, back):
        dx, dy, dz = lax.rem(t, NX), lax.div(t, NX), dz_of(k, p)
        if back:
            return away(NX - dx, NZ - dz, dy)
        return away(dx, dz, dy)

    def each_peer(fn, chunks=CH):
        for k in chunks:
            if k == 0:
                fn(0, 1, jnp.int32(0))
                lo = 1
            else:
                lo = 0

            @pl.loop(lo, 8)
            def _(t):
                fn(k, 0, t)
                fn(k, 1, t)

    def quad(j):
        return lax.rem(yl + j // 2, 2) * 2 + lax.rem(core + j % 2, 2)

    def dev(g, i):
        return {"group": g, "inner": i}

    def fetch(kind, n):
        src = (tok_all, og_all)[kind]
        rows = pl.ds(n * (RAW // 4), RAW // 4)
        return pltpu.make_async_copy(src.at[rows], raw.at[kind, rows], tsem.at[kind, n])

    router_copy = pltpu.make_async_copy(router_all, router, wsem.at[2])
    for n in range(4):
        fetch(0, n).start()
    router_copy.start()
    for n in range(4):
        fetch(1, n).start()
    barrier = pltpu.get_barrier_semaphore()

    def greet(k, p, t):
        i2, g2 = target(k, p, t, False)
        pl.semaphore_signal(barrier, inc=1, device_id=dev(g2, i2))

    each_peer(greet)
    for j in range(1, 4):
        pl.semaphore_signal(barrier, inc=1, device_id=dev(quad(j), inner))

    wcopy_in = pltpu.make_async_copy(w_in, win, wsem.at[0])
    wcopy_out = pltpu.make_async_copy(w_out, wout, wsem.at[1])
    wcopy_in.start()
    wcopy_out.start()

    wide[RAW:, :] = jnp.zeros((PAD * 32 - RAW, 128), F32)

    def extract(kind, dst):
        for n in range(4):
            fetch(kind, n).wait()
            rows = slice(n * (RAW // 4), (n + 1) * (RAW // 4))
            wide[rows, :] = raw[kind, rows, :].astype(F32)
        for a in range(8):
            dst[:, a * 128 : (a + 1) * 128] = wide[
                pl.ds(a * 4 + group, PAD, stride=32), :
            ].astype(BF)

    with scope("extract0"):
        extract(0, tok)
    router_copy.wait()
    logits = dot(tok[...], router[...], 1, 0)
    keep = lax.broadcasted_iota(jnp.int32, (PAD, S), 0) < TOK
    top = jnp.max(jnp.where(keep, logits, -jnp.inf), axis=0, keepdims=True)
    e = jnp.where(keep, jnp.exp(jnp.where(keep, logits - top, 0.0)), 0.0)
    disp[...] = e / jnp.sum(e, axis=0, keepdims=True)
    e = jnp.exp(logits - jnp.max(logits, axis=1, keepdims=True))
    comb[...] = e / jnp.sum(e, axis=1, keepdims=True)

    def to_tiles(kind, weights, values):
        flipped = weights.T.astype(BF)
        val = dot(flipped, values[...], 1, 0)
        for a in range(8):
            fs[pl.ds(a, S, stride=8), :] = val[:, a * 128 : (a + 1) * 128]
        sbuf[kind] = fs[...].reshape(S, 8, 128).astype(BF)

    def send_stage(st):
        kind, ex = st // 2, st % 2

        def send(k, p, t):
            i2, g2 = target(k, p, t, False)
            pltpu.make_async_remote_copy(
                sbuf.at[kind, i2 * 2 + ex],
                x.at[st, 0, slot_of(k, p, t)],
                send1.at[st],
                recv1.at[st, CH.index(k) // 2],
                device_id=dev(g2, i2),
            ).start()

        pltpu.make_async_copy(
            sbuf.at[kind, inner * 2 + ex], x.at[st, 0, SELF], recv1.at[st, 0]
        ).start()
        each_peer(send)

    with scope("tiles0"):
        to_tiles(0, disp[...], tok)
    with scope("barrier"):
        pl.semaphore_wait(barrier, NI - 1 + 3)
    with scope("send0"):
        send_stage(0)
        send_stage(1)
    with scope("extract1"):
        extract(1, og)
    with scope("tiles1"):
        to_tiles(1, comb[...], og)
    with scope("send1"):
        send_stage(2)
        send_stage(3)

    def part(st, q, h):
        return x.at[st, q, pl.ds(h * 32, 32)]

    def ycopy(st, h):
        return pltpu.make_async_remote_copy(
            part(st, 0, h), part(st, 1, h), ysend.at[st, h], yrecv.at[st, h],
            device_id=dev(quad(2), inner),
        )

    def ccopy(st, q, h):
        return pltpu.make_async_remote_copy(
            part(st, q, h), part(st, q + 2, h), csend.at[st, q, h], crecv.at[st, q, h],
            device_id=dev(quad(1), inner),
        )

    def forward_a(st, h):
        with scope(f"fwdA{st}{h}"):
            pltpu.make_async_copy(part(st, 0, h), part(st, 0, h), recv1.at[st, h]).wait()
        ycopy(st, h).start()
        ccopy(st, 0, h).start()

    def forward_b(st, h):
        with scope(f"fwdB{st}{h}"):
            ycopy(st, h).wait_recv()
        ccopy(st, 1, h).start()

    def to_rows(st, q):
        fs[0:512, :] = x[st, q].astype(F32).reshape(512, 128)
        for a in range(8):
            lhs[st, q * 64 : (q + 1) * 64, a * 128 : (a + 1) * 128] = fs[
                pl.ds(a, 64, stride=8), :
            ].astype(BF)

    def rows_ab(st):
        to_rows(st, 0)
        to_rows(st, 1)

    def rows_cd(st):
        for q in range(2):
            with scope(f"settle{st}{q}"):
                for h in range(2):
                    ccopy(st, q, h).wait_recv()
            to_rows(st, q + 2)

    def scatter_rows(dst, n, val):
        for q in range(4):
            for a in range(NT // 128):
                dst[pl.ds(q * 512 + n * (NT // 128) + a, 64, stride=8), :] = val[
                    q * 64 : (q + 1) * 64, a * 128 : (a + 1) * 128
                ]

    sums = (s0, s1, s2, s3)
    c0 = math.sqrt(2.0 / math.pi)

    def pre(ex):
        for n in range(D // NT):
            cols = slice(n * NT, (n + 1) * NT)
            h = dot(lhs[ex], win[ex, :, cols], 1, 0)
            h2 = h * h
            th = jnp.tanh(c0 * (h + 0.044715 * h2 * h))
            half = 0.5 * (1.0 + th)
            act[:, cols] = (h * half).astype(BF)
            dg[ex, :, cols] = half + 0.5 * h * (1.0 - th * th) * (
                c0 * (1.0 + (3.0 * 0.044715) * h2)
            )

    def out(ex):
        for n in range(D // NT):
            scatter_rows(sums[ex], n, dot(act[...], wout[ex, :, n * NT : (n + 1) * NT], 1, 0))

    def act_grad(ex):
        for n in range(D // NT):
            cols = slice(n * NT, (n + 1) * NT)
            ag = dot(lhs[2 + ex], wout[ex, cols, :], 1, 1)
            pg[:, cols] = (dg[ex, :, cols] * ag).astype(BF)

    def back(ex):
        for n in range(D // NT):
            scatter_rows(
                sums[2 + ex], n, dot(pg[...], win[ex, n * NT : (n + 1) * NT, :], 1, 1)
            )

    def pcopy(st, q):
        return pltpu.make_async_remote_copy(
            cbuf.at[st, q], pbuf.at[st, q], psend.at[st, q], precv.at[st, q],
            device_id=dev(quad(1), inner),
        )

    def bcopy(st, h):
        sel = pl.ds(h * 32, 32)
        return pltpu.make_async_remote_copy(
            ybuf.at[st, sel], rbuf.at[st, sel], bsend.at[st, h], brecv.at[st, h],
            device_id=dev(quad(2), inner),
        )

    def rows_of(st, q, h):
        lo = q * 512 + h * 256
        return sums[st][lo : lo + 256, :].reshape(32, 8, 128)

    def reduce_1(st):
        with scope(f"reduce1_{st}"):
            for q in (1, 0):
                cbuf[st, q] = (
                    sums[st][(q + 2) * 512 : (q + 3) * 512, :].reshape(64, 8, 128).astype(BF)
                )
                pcopy(st, q).start()

    def reduce_2(st):
        with scope(f"reduce2_{st}"):
            pcopy(st, 1).wait_recv()
            for h in range(2):
                sel = pl.ds(h * 32, 32)
                ybuf[st, sel] = (rows_of(st, 1, h) + pbuf[st, 1, sel].astype(F32)).astype(BF)
                bcopy(st, h).start()
            pcopy(st, 0).wait_recv()

    def reduce_3(st, h):
        kind, ex = st // 2, st % 2
        sel = pl.ds(h * 32, 32)
        with scope(f"reduce3_{st}{h}"):
            bcopy(st, h).wait_recv()
        abuf[st, sel] = (
            rows_of(st, 0, h) + pbuf[st, 0, sel].astype(F32) + rbuf[st, sel].astype(F32)
        ).astype(BF)
        if h == 0:
            pltpu.make_async_copy(
                abuf.at[st, SELF], so.at[kind, inner, ex], arecv.at[kind]
            ).start()

        def send(k, p, t):
            i2, g2 = target(k, p, t, True)
            pltpu.make_async_remote_copy(
                abuf.at[st, slot_of(k, p, t)], so.at[kind, inner, ex], asend.at[st],
                arecv.at[kind], device_id=dev(g2, i2),
            ).start()

        with scope("a2a"):
            each_peer(send, HALVES[h])

    forward_a(0, 0)
    forward_a(0, 1)
    forward_a(1, 0)
    forward_b(0, 0)
    forward_a(1, 1)
    forward_b(0, 1)
    with scope("rows"):
        rows_ab(0)
    forward_a(2, 0)
    with scope("rows"):
        rows_cd(0)
    wcopy_in.wait()
    wcopy_out.wait()
    with scope("pre"):
        pre(0)
    forward_b(1, 0)
    forward_a(2, 1)
    forward_b(1, 1)
    with scope("out"):
        out(0)
    reduce_1(0)
    forward_a(3, 0)
    with scope("rows"):
        rows_ab(1)
        rows_cd(1)
    reduce_2(0)
    with scope("pre"):
        pre(1)
    forward_b(2, 0)
    forward_a(3, 1)
    with scope("out"):
        out(1)
    reduce_1(1)
    forward_b(2, 1)
    with scope("rows"):
        rows_ab(2)
        rows_cd(2)
    reduce_2(1)
    with scope("actgrad"):
        act_grad(0)
    forward_b(3, 0)
    with scope("back"):
        back(0)
    reduce_1(2)
    forward_b(3, 1)
    with scope("rows"):
        rows_ab(3)
    reduce_3(0, 0)
    with scope("rows"):
        rows_cd(3)
    reduce_2(2)
    with scope("actgrad"):
        act_grad(1)
    reduce_3(0, 1)
    with scope("back"):
        back(1)
    reduce_1(3)
    reduce_3(1, 0)
    reduce_2(3)
    reduce_3(1, 1)
    for st in (2, 3):
        for h in range(2):
            reduce_3(st, h)

    def gather_rows(kind):
        pltpu.make_async_copy(so.at[kind], so.at[kind], arecv.at[kind]).wait()
        fs[...] = so[kind].astype(F32).reshape(1024, 128)
        for a in range(8):
            so_m[kind, :, a * 128 : (a + 1) * 128] = fs[pl.ds(a, S, stride=8), :].astype(BF)

    with scope("gather0"):
        gather_rows(0)
    cg = dot(og[...], so_m[0], 1, 1)
    cw = comb[...]
    lg = cw * (cg - jnp.sum(cw * cg, axis=1, keepdims=True))
    with scope("gather1"):
        gather_rows(1)
    dgr = dot(tok[...], so_m[1], 1, 1)
    dw = disp[...]
    lg = lg + dw * (dgr - jnp.sum(dw * dgr, axis=0, keepdims=True))
    lb = lg.astype(BF)
    rgo[...] = dot(tok[...], lb, 0, 0).reshape(NI, 2, 8, 128)
    rgs[...] = rgo[:, pl.ds(1 - core, 1)].reshape(NI, 8, 128).astype(BF)

    gcopy = pltpu.make_async_remote_copy(
        rgs, rgp, gsend, grecv, device_id=dev(quad(1), inner)
    )
    gcopy.start()
    with scope("tg"):
        tg = dot(dw.astype(BF), so_m[1], 1, 0) + dot(lb, router[...], 1, 1)
        for g in range(4):
            tgb[g] = tg[:, g * 256 : (g + 1) * 256].astype(BF)

    def tcopy(j):
        g2 = quad(j)
        return pltpu.make_async_remote_copy(
            tgb.at[g2], land.at[group], tsend.at[j], trecv.at[j], device_id=dev(g2, inner)
        )

    for j in (2, 3, 1):
        tcopy(j).start()
    mine = pltpu.make_async_copy(tgb.at[group], land.at[group], tsend.at[0])
    mine.start()

    with scope("wait_g"):
        gcopy.wait_recv()
    rgb[...] = (
        rgo[:, pl.ds(core, 1)].reshape(NI, 8, 128) + rgp[...].astype(F32)
    ).astype(BF)

    def send_router(k, p, t):
        i2, g2 = target(k, p, t, False)
        pltpu.make_async_remote_copy(
            rgb.at[i2], rr.at[slot_of(k, p, t)], rsend, rrecv, device_id=dev(g2, i2)
        ).start()

    with scope("send_router"):
        pltpu.make_async_copy(rgb.at[inner], rr.at[SELF], rrecv).start()
        each_peer(send_router)

    with scope("wait_router"):
        pltpu.make_async_copy(rr, rr, rrecv).wait()
    qs[0] = jnp.sum(rr[...].astype(F32), axis=0)

    def qcopy(j):
        return pltpu.make_async_remote_copy(
            qs.at[0], qs.at[j], qsend.at[j], qrecv.at[j], device_id=dev(quad(j), inner)
        )

    for j in (2, 3, 1):
        qcopy(j).start()
    with scope("wait_tg"):
        for j in range(1, 4):
            tcopy(j).wait()
        mine.wait()
    with scope("wait_q"):
        for j in range(1, 4):
            qcopy(j).wait()
    rg[pl.ds(core * 8, 8), :] = qs[0] + qs[2]
    rg[pl.ds((1 - core) * 8, 8), :] = qs[1] + qs[3]

    for st in range(4):
        pltpu.make_async_copy(
            x.at[st, 0, pl.ds(1, NI - 1)], x.at[st, 0, pl.ds(1, NI - 1)], send1.at[st]
        ).wait()
        pltpu.make_async_copy(
            abuf.at[st, pl.ds(1, NI - 1)], abuf.at[st, pl.ds(1, NI - 1)], asend.at[st]
        ).wait()
        for h in range(2):
            ycopy(st, h).wait_send()
            bcopy(st, h).wait_send()
            for q in range(2):
                ccopy(st, q, h).wait_send()
        for q in range(2):
            pcopy(st, q).wait_send()
    gcopy.wait_send()
    pltpu.make_async_copy(rr.at[pl.ds(1, NI - 1)], rr.at[pl.ds(1, NI - 1)], rsend).wait()


def finish(land, rg, tg_out, rg_out, wide):
    for g in range(4):
        for a in range(2):
            wide[pl.ds(a * 4 + g, PAD, stride=8), :] = land[
                g, :, a * 128 : (a + 1) * 128
            ].astype(F32)
    tg_out[...] = wide[: TOK * 8, :].astype(BF)
    rg_out[...] = rg[...]


def local(tokens, output_grad, router, weight_in, weight_out):
    def as_stored(a):
        a = a.transpose(1, 0, 2).reshape(TOK, 4, 8, 128).transpose(0, 2, 1, 3)
        return a.reshape(RAW, 128)

    dma = pltpu.SemaphoreType.DMA
    vm = pl.BlockSpec(memory_space=pltpu.VMEM)
    hbm = pl.BlockSpec(memory_space=pl.ANY)
    land, rg = pl.pallas_call(
        kernel,
        name="moe_backward",
        out_shape=(pltpu.VMEM((4, PAD, 256), BF), pltpu.VMEM((16, S), F32)),
        in_specs=[hbm, hbm, hbm, hbm, hbm],
        out_specs=(vm, vm),
        scratch_shapes=[
            pltpu.VMEM((2, RAW, 128), BF),
            pltpu.VMEM((PAD * 32, 128), F32),
            pltpu.VMEM((PAD, D), BF),
            pltpu.VMEM((PAD, D), BF),
            pltpu.VMEM((D, S), BF),
            pltpu.VMEM((2, D, D), BF),
            pltpu.VMEM((2, D, D), BF),
            pltpu.VMEM((PAD, S), F32),
            pltpu.VMEM((PAD, S), F32),
            pltpu.VMEM((2, S, 8, 128), BF),
            pltpu.VMEM((4, 4, NI, 8, 128), BF),
            pltpu.VMEM((1024, 128), F32),
            pltpu.VMEM((4, 256, D), BF),
            pltpu.VMEM((2, 256, D), F32),
            pltpu.VMEM((256, D), BF),
            pltpu.VMEM((256, D), BF),
            pltpu.VMEM((2048, 128), F32),
            pltpu.VMEM((2048, 128), F32),
            pltpu.VMEM((2048, 128), F32),
            pltpu.VMEM((2048, 128), F32),
            pltpu.VMEM((4, 2, NI, 8, 128), BF),
            pltpu.VMEM((4, 2, NI, 8, 128), BF),
            pltpu.VMEM((4, NI, 8, 128), BF),
            pltpu.VMEM((4, NI, 8, 128), BF),
            pltpu.VMEM((4, NI, 8, 128), BF),
            pltpu.VMEM((2, NI, 2, 8, 128), BF),
            pltpu.VMEM((2, S, D), BF),
            pltpu.VMEM((NI, 2, 8, 128), F32),
            pltpu.VMEM((NI, 8, 128), BF),
            pltpu.VMEM((NI, 8, 128), BF),
            pltpu.VMEM((NI, 8, 128), BF),
            pltpu.VMEM((NI, 8, 128), BF),
            pltpu.VMEM((4, PAD, 256), BF),
            pltpu.VMEM((4, 8, 128), F32),
            dma((2, 4)),
            dma((3,)),
            dma((4,)), dma((4, 2)),
            dma((4, 2)), dma((4, 2)),
            dma((4, 2, 2)), dma((4, 2, 2)),
            dma((4, 2)), dma((4, 2)),
            dma((4, 2)), dma((4, 2)),
            dma((4,)), dma((2,)),
            dma, dma,
            dma, dma,
            dma((4,)), dma((4,)),
            dma((4,)), dma((4,)),
        ],
        compiler_params=pltpu.CompilerParams(
            collective_id=0, has_side_effects=True, vmem_limit_bytes=58 * 1024 * 1024
        ),
    )(as_stored(tokens), as_stored(output_grad), router, weight_in, weight_out)
    tg, rg = pl.pallas_call(
        finish,
        name="moe_finish",
        out_shape=(
            jax.ShapeDtypeStruct((TOK * 8, 128), BF),
            jax.ShapeDtypeStruct((16, S), F32),
        ),
        in_specs=[vm, vm],
        out_specs=(vm, vm),
        scratch_shapes=[pltpu.VMEM((PAD * 8, 128), F32)],
        compiler_params=pltpu.CompilerParams(vmem_limit_bytes=16 * 1024 * 1024),
    )(land, rg)
    tg = tg.reshape(TOK, 2, 4, 128).transpose(2, 0, 1, 3).reshape(4, TOK, 256)
    return tg, rg


def solution(mesh):
    return jax.shard_map(
        local,
        mesh=mesh,
        in_specs=(
            P("inner", None, None),
            P("inner", None, None),
            P(),
            P("inner", None, "group"),
            P("inner", "group", None),
        ),
        out_specs=(P("inner", None, "group"), P("inner", None)),
        check_vma=False,
    )
```

time: 76.2 us -> 67.6 us (0.89)
  Pallas kernels: 72.1 us -> 66.5 us
  local copies, waits for them, and re-layouts: 3.18 us -> 0 us
    pallas_call x1 -> x2, Pallas kernels: 72.1 us -> 66.5 us  [the longest x1 65.5 us: local(): pl.pallas_call(kernel, name='moe_backward', out_shape=(pltpu.VMEM((4, PAD...]
    unnamed x2 -> x0, local copies, waits for them, and re-layouts: 3.18 us -> none
where the time goes in v3:
time: 67.6 us; the launch traced here: 67.1 us
  Pallas kernels  66.5 us (98%)
    pallas_call x1, Pallas kernels, local(): pl.pallas_call(kernel, name='moe_backward', out_shape=(pltpu.VMEM((4, PAD...  65.5 us

profile of v3, /device:TPU:1, one launch (start us, length us, event | category | flops | bytes accessed | tf_op | source)
XLA Modules:
  0.0 67.1 jit_solution(17828340726259375931)
XLA Ops:
  0.6 65.5 %moe_backward.1 = (bf16[4,208,256]{2,1,0:T(8,128)(2,1)S(1)}, f32[16,128]{1,0:T(8,128)S(1)}) custom-call(bf16[6272,128]{1,0:T(8,128)(2,1)} %bitcast.19, bf16[6272,128]{1,0:T(8,128)(2,1)} %bitcast.20, bf16[1024,128]{1,0:T(8,128)(2,1)} %router_all.1, bf16[2,1024,1024]{2,1,0:T(8,128)(2,1)} %w_in.1, bf16[2,1024,1024]{2,1,0:T(8,128)(2,1)} %w_out.1), custom_call_target="tpu_custom_call" | custom-call | tf_op jit(solution)/shard_map/moe_backward/pallas_call | solution.py:496
  66.1 1.0 %moe_finish.1 = (bf16[1568,128]{1,0:T(8,128)(2,1)}, f32[16,128]{1,0:T(8,128)}) custom-call(bf16[4,208,256]{2,1,0:T(8,128)(2,1)S(1)} %get-tuple-element.6.land, f32[16,128]{1,0:T(8,128)S(1)} %get-tuple-element.7.rg), custom_call_target="tpu_custom_call" | custom-call | tf_op jit(solution)/shard_map/moe_finish/pallas_call | solution.py:554

commit v4 on v3

--- a/solution.py
+++ b/solution.py
@@ -18,33 +18,23 @@
 S = 128
 RAW = TOK * 32
 NT = 512
-CH = (3, 0, 2, 1)
-HALVES = ((3, 0), (2, 1))
-SELF = 16
+NEAR, FAR = 0, 1
+DZ = ((0, 1, 7, 2), (4, 3, 5, 6))
+SELF = 0
 
 
 def scope(name):
     return contextlib.nullcontext()
 
 
-def slot_of(k, p, t):
-    return CH.index(k) * 16 + t * 2 + p
-
-
-def dz_of(k, p):
-    if k == 0:
-        return 4 * p
-    return k if p == 0 else NZ - k
-
-
 def dot(a, b, ca, cb):
     return lax.dot_general(a, b, (((ca,), (cb,)), ((), ())), preferred_element_type=F32)
 
 
 def kernel(
     tok_all, og_all, router_all, w_in, w_out,
-    land, rg,
-    raw, wide, tok, og, router, win, wout, disp, comb, sbuf, x, fs, lhs, dg, act, pg, s0, s1, s2, s3,
+    tg_out, rg,
+    raw, wide, tok, og, router, land, win, wout, disp, comb, sbuf, x, fs, lhs, dg, act, pg, s0, s1, s2, s3,
     cbuf, pbuf, ybuf, rbuf, abuf, so, so_m, rgo, rgs, rgp, rgb, rr, tgb, qs,
     tsem, wsem, send1, recv1, ysend, yrecv, csend, crecv,
     psend, precv, bsend, brecv, asend, arecv,
@@ -58,29 +48,27 @@
     yl = lax.div(group, 2)
     core = lax.rem(group, 2)
 
-    def away(dx, dz, dy):
-        x2, z2 = lax.rem(xc + dx, NX), lax.rem(zc + dz, NZ)
-        y2, l2 = lax.rem(yh + dy, 2), lax.rem(yl + dy, 2)
-        return (x2 * NZ + z2) * NY + y2, l2 * 2 + core
-
-    def target(k, p, t, back):
-        dx, dy, dz = lax.rem(t, NX), lax.div(t, NX), dz_of(k, p)
-        if back:
-            return away(NX - dx, NZ - dz, dy)
-        return away(dx, dz, dy)
-
-    def each_peer(fn, chunks=CH):
-        for k in chunks:
-            if k == 0:
-                fn(0, 1, jnp.int32(0))
-                lo = 1
-            else:
-                lo = 0
-
-            @pl.loop(lo, 8)
-            def _(t):
-                fn(k, 0, t)
-                fn(k, 1, t)
+    ahead = [lax.rem(zc + dz, NZ) * NY for dz in range(NZ)]
+    behind = [lax.rem(zc + NZ - dz, NZ) * NY for dz in range(NZ)]
+
+    def each_peer(fn, half, back=False):
+        def at(t, js):
+            dx, dy = lax.rem(t, NX), lax.div(t, NX)
+            x2 = lax.rem(xc + (NX - dx if back else dx), NX) * (NY * NZ)
+            y2, l2 = lax.rem(yh + dy, 2), lax.rem(yl + dy, 2)
+            base, g2 = x2 + y2, l2 * 2 + core
+            for j in js:
+                dz = DZ[half][j]
+                fn(base + (behind if back else ahead)[dz], g2, half * 32 + j * 8 + t)
+
+        lo = 0
+        if half == NEAR:
+            at(jnp.int32(0), (1, 2, 3))
+            lo = 1
+
+        @pl.loop(lo, 8)
+        def _(t):
+            at(t, (0, 1, 2, 3))
 
     def quad(j):
         return lax.rem(yl + j // 2, 2) * 2 + lax.rem(core + j % 2, 2)
@@ -101,11 +89,11 @@
         fetch(1, n).start()
     barrier = pltpu.get_barrier_semaphore()
 
-    def greet(k, p, t):
-        i2, g2 = target(k, p, t, False)
+    def greet(i2, g2, r):
         pl.semaphore_signal(barrier, inc=1, device_id=dev(g2, i2))
 
-    each_peer(greet)
+    each_peer(greet, FAR)
+    each_peer(greet, NEAR)
     for j in range(1, 4):
         pl.semaphore_signal(barrier, inc=1, device_id=dev(quad(j), inner))
 
@@ -144,51 +132,46 @@
             fs[pl.ds(a, S, stride=8), :] = val[:, a * 128 : (a + 1) * 128]
         sbuf[kind] = fs[...].reshape(S, 8, 128).astype(BF)
 
-    def send_stage(st):
+    def send_stage(st, h):
         kind, ex = st // 2, st % 2
 
-        def send(k, p, t):
-            i2, g2 = target(k, p, t, False)
+        def send(i2, g2, r):
             pltpu.make_async_remote_copy(
-                sbuf.at[kind, i2 * 2 + ex],
-                x.at[st, 0, slot_of(k, p, t)],
-                send1.at[st],
-                recv1.at[st, CH.index(k) // 2],
+                sbuf.at[kind, i2 * 2 + ex], x.at[st, 0, r], send1, recv1.at[st, h],
                 device_id=dev(g2, i2),
             ).start()
 
-        pltpu.make_async_copy(
-            sbuf.at[kind, inner * 2 + ex], x.at[st, 0, SELF], recv1.at[st, 0]
-        ).start()
-        each_peer(send)
+        if h == NEAR:
+            pltpu.make_async_copy(
+                sbuf.at[kind, inner * 2 + ex], x.at[st, 0, SELF], recv1.at[st, h]
+            ).start()
+        each_peer(send, h)
 
     with scope("tiles0"):
         to_tiles(0, disp[...], tok)
-    with scope("barrier"):
-        pl.semaphore_wait(barrier, NI - 1 + 3)
-    with scope("send0"):
-        send_stage(0)
-        send_stage(1)
     with scope("extract1"):
         extract(1, og)
     with scope("tiles1"):
         to_tiles(1, comb[...], og)
-    with scope("send1"):
-        send_stage(2)
-        send_stage(3)
+    with scope("barrier"):
+        pl.semaphore_wait(barrier, NI - 1 + 3)
+    with scope("send"):
+        for st in range(4):
+            for h in (NEAR, FAR) if st == 0 else (FAR, NEAR):
+                send_stage(st, h)
 
     def part(st, q, h):
         return x.at[st, q, pl.ds(h * 32, 32)]
 
     def ycopy(st, h):
         return pltpu.make_async_remote_copy(
-            part(st, 0, h), part(st, 1, h), ysend.at[st, h], yrecv.at[st, h],
+            part(st, 0, h), part(st, 1, h), ysend, yrecv.at[st, h],
             device_id=dev(quad(2), inner),
         )
 
     def ccopy(st, q, h):
         return pltpu.make_async_remote_copy(
-            part(st, q, h), part(st, q + 2, h), csend.at[st, q, h], crecv.at[st, q, h],
+            part(st, q, h), part(st, q + 2, h), csend, crecv.at[st, q],
             device_id=dev(quad(1), inner),
         )
 
@@ -217,8 +200,8 @@
     def rows_cd(st):
         for q in range(2):
             with scope(f"settle{st}{q}"):
-                for h in range(2):
-                    ccopy(st, q, h).wait_recv()
+                done = x.at[st, q + 2]
+                pltpu.make_async_copy(done, done, crecv.at[st, q]).wait()
             to_rows(st, q + 2)
 
     def scatter_rows(dst, n, val):
@@ -261,14 +244,14 @@
 
     def pcopy(st, q):
         return pltpu.make_async_remote_copy(
-            cbuf.at[st, q], pbuf.at[st, q], psend.at[st, q], precv.at[st, q],
+            cbuf.at[st, q], pbuf.at[st, q], psend, precv.at[st, q],
             device_id=dev(quad(1), inner),
         )
 
     def bcopy(st, h):
         sel = pl.ds(h * 32, 32)
         return pltpu.make_async_remote_copy(
-            ybuf.at[st, sel], rbuf.at[st, sel], bsend.at[st, h], brecv.at[st, h],
+            ybuf.at[st, sel], rbuf.at[st, sel], bsend, brecv.at[st, h],
             device_id=dev(quad(2), inner),
         )
 
@@ -287,97 +270,96 @@
     def reduce_2(st):
         with scope(f"reduce2_{st}"):
             pcopy(st, 1).wait_recv()
-            for h in range(2):
+            for h in (FAR, NEAR):
                 sel = pl.ds(h * 32, 32)
                 ybuf[st, sel] = (rows_of(st, 1, h) + pbuf[st, 1, sel].astype(F32)).astype(BF)
                 bcopy(st, h).start()
-            pcopy(st, 0).wait_recv()
 
     def reduce_3(st, h):
         kind, ex = st // 2, st % 2
         sel = pl.ds(h * 32, 32)
         with scope(f"reduce3_{st}{h}"):
+            if h == FAR:
+                pcopy(st, 0).wait_recv()
             bcopy(st, h).wait_recv()
         abuf[st, sel] = (
             rows_of(st, 0, h) + pbuf[st, 0, sel].astype(F32) + rbuf[st, sel].astype(F32)
         ).astype(BF)
-        if h == 0:
+        if h == NEAR:
             pltpu.make_async_copy(
                 abuf.at[st, SELF], so.at[kind, inner, ex], arecv.at[kind]
             ).start()
 
-        def send(k, p, t):
-            i2, g2 = target(k, p, t, True)
+        def send(i2, g2, r):
             pltpu.make_async_remote_copy(
-                abuf.at[st, slot_of(k, p, t)], so.at[kind, inner, ex], asend.at[st],
-                arecv.at[kind], device_id=dev(g2, i2),
+                abuf.at[st, r], so.at[kind, inner, ex], asend, arecv.at[kind],
+                device_id=dev(g2, i2),
             ).start()
 
         with scope("a2a"):
-            each_peer(send, HALVES[h])
-
-    forward_a(0, 0)
-    forward_a(0, 1)
-    forward_a(1, 0)
-    forward_b(0, 0)
-    forward_a(1, 1)
-    forward_b(0, 1)
+            each_peer(send, h, back=True)
+
+    forward_a(0, NEAR)
+    forward_a(0, FAR)
+    forward_a(1, NEAR)
+    forward_b(0, NEAR)
+    forward_a(1, FAR)
+    forward_b(0, FAR)
     with scope("rows"):
         rows_ab(0)
-    forward_a(2, 0)
+    forward_a(2, NEAR)
     with scope("rows"):
         rows_cd(0)
     wcopy_in.wait()
     wcopy_out.wait()
     with scope("pre"):
         pre(0)
-    forward_b(1, 0)
-    forward_a(2, 1)
-    forward_b(1, 1)
+    forward_b(1, NEAR)
+    forward_a(2, FAR)
+    forward_b(1, FAR)
     with scope("out"):
         out(0)
     reduce_1(0)
-    forward_a(3, 0)
+    forward_a(3, NEAR)
     with scope("rows"):
         rows_ab(1)
         rows_cd(1)
+    forward_a(3, FAR)
     reduce_2(0)
     with scope("pre"):
         pre(1)
-    forward_b(2, 0)
-    forward_a(3, 1)
+    forward_b(2, NEAR)
+    forward_b(2, FAR)
     with scope("out"):
         out(1)
     reduce_1(1)
-    forward_b(2, 1)
     with scope("rows"):
         rows_ab(2)
         rows_cd(2)
-    reduce_2(1)
     with scope("actgrad"):
         act_grad(0)
-    forward_b(3, 0)
+    forward_b(3, NEAR)
+    reduce_2(1)
+    forward_b(3, FAR)
     with scope("back"):
         back(0)
     reduce_1(2)
-    forward_b(3, 1)
     with scope("rows"):
         rows_ab(3)
-    reduce_3(0, 0)
-    with scope("rows"):
         rows_cd(3)
-    reduce_2(2)
+    reduce_3(0, FAR)
     with scope("actgrad"):
         act_grad(1)
-    reduce_3(0, 1)
+    reduce_2(2)
+    reduce_3(0, NEAR)
     with scope("back"):
         back(1)
     reduce_1(3)
-    reduce_3(1, 0)
+    reduce_3(1, FAR)
     reduce_2(3)
-    reduce_3(1, 1)
+    reduce_3(1, NEAR)
     for st in (2, 3):
-        for h in range(2):
+        for h in (FAR, NEAR):
             reduce_3(st, h)
 
     def gather_rows(kind):
@@ -412,12 +394,12 @@
     def tcopy(j):
         g2 = quad(j)
         return pltpu.make_async_remote_copy(
-            tgb.at[g2], land.at[group], tsend.at[j], trecv.at[j], device_id=dev(g2, inner)
+            tgb.at[g2], land.at[group], tsend, trecv, device_id=dev(g2, inner)
         )
 
     for j in (2, 3, 1):
         tcopy(j).start()
-    mine = pltpu.make_async_copy(tgb.at[group], land.at[group], tsend.at[0])
+    mine = pltpu.make_async_copy(tgb.at[group], land.at[group], trecv)
     mine.start()
 
     with scope("wait_g"):
@@ -426,15 +408,25 @@
         rgo[:, pl.ds(core, 1)].reshape(NI, 8, 128) + rgp[...].astype(F32)
     ).astype(BF)
 
-    def send_router(k, p, t):
-        i2, g2 = target(k, p, t, False)
+    def send_router(i2, g2, r):
         pltpu.make_async_remote_copy(
-            rgb.at[i2], rr.at[slot_of(k, p, t)], rsend, rrecv, device_id=dev(g2, i2)
+            rgb.at[i2], rr.at[r], rsend, rrecv, device_id=dev(g2, i2)
         ).start()
 
     with scope("send_router"):
+        each_peer(send_router, FAR)
+        each_peer(send_router, NEAR)
         pltpu.make_async_copy(rgb.at[inner], rr.at[SELF], rrecv).start()
-        each_peer(send_router)
+
+    with scope("wait_tg"):
+        pltpu.make_async_copy(land, land, trecv).wait()
+    with scope("tg_out"):
+        for g in range(4):
+            for a in range(2):
+                wide[pl.ds(a * 4 + g, PAD, stride=8), :] = land[
+                    g, :, a * 128 : (a + 1) * 128
+                ].astype(F32)
+        tg_out[...] = wide[: TOK * 8, :].astype(BF)
 
     with scope("wait_router"):
         pltpu.make_async_copy(rr, rr, rrecv).wait()
@@ -442,47 +434,44 @@
 
     def qcopy(j):
         return pltpu.make_async_remote_copy(
-            qs.at[0], qs.at[j], qsend.at[j], qrecv.at[j], device_id=dev(quad(j), inner)
+            qs.at[0], qs.at[j], qsend, qrecv, device_id=dev(quad(j), inner)
         )
 
     for j in (2, 3, 1):
         qcopy(j).start()
-    with scope("wait_tg"):
-        for j in range(1, 4):
-            tcopy(j).wait()
-        mine.wait()
     with scope("wait_q"):
-        for j in range(1, 4):
-            qcopy(j).wait()
+        pltpu.make_async_copy(qs.at[pl.ds(1, 3)], qs.at[pl.ds(1, 3)], qrecv).wait()
     rg[pl.ds(core * 8, 8), :] = qs[0] + qs[2]
     rg[pl.ds((1 - core) * 8, 8), :] = qs[1] + qs[3]
 
-    for st in range(4):
+    with scope("end"):
+        for ref, sem in (
+            (x.at[:, 0, pl.ds(1, NI - 1)], send1),
+            (abuf.at[:, pl.ds(1, NI - 1)], asend),
+            (x.at[:, 0], ysend),
+            (x.at[:, pl.ds(0, 2)], csend),
+            (pbuf, psend),
+            (rbuf, bsend),
+            (rgp, gsend),
+            (rr.at[pl.ds(1, NI - 1)], rsend),
+            (land.at[pl.ds(0, 3)], tsend),
+            (qs.at[pl.ds(1, 3)], qsend),
+        ):
+            pltpu.make_async_copy(ref, ref, sem).wait()
+
+
+def finish(tg, rg, tg_out, rg_out, sem):
+    rows = TOK * 8 // 4
+    copies = [
         pltpu.make_async_copy(
-            x.at[st, 0, pl.ds(1, NI - 1)], x.at[st, 0, pl.ds(1, NI - 1)], send1.at[st]
-        ).wait()
-        pltpu.make_async_copy(
-            abuf.at[st, pl.ds(1, NI - 1)], abuf.at[st, pl.ds(1, NI - 1)], asend.at[st]
-        ).wait()
-        for h in range(2):
-            ycopy(st, h).wait_send()
-            bcopy(st, h).wait_send()
-            for q in range(2):
-                ccopy(st, q, h).wait_send()
-        for q in range(2):
-            pcopy(st, q).wait_send()
-    gcopy.wait_send()
-    pltpu.make_async_copy(rr.at[pl.ds(1, NI - 1)], rr.at[pl.ds(1, NI - 1)], rsend).wait()
-
-
-def finish(land, rg, tg_out, rg_out, wide):
-    for g in range(4):
-        for a in range(2):
-            wide[pl.ds(a * 4 + g, PAD, stride=8), :] = land[
-                g, :, a * 128 : (a + 1) * 128
-            ].astype(F32)
-    tg_out[...] = wide[: TOK * 8, :].astype(BF)
-    rg_out[...] = rg[...]
+            tg.at[pl.ds(n * rows, rows)], tg_out.at[pl.ds(n * rows, rows)], sem.at[n]
+        )
+        for n in range(4)
+    ] + [pltpu.make_async_copy(rg, rg_out, sem.at[4])]
+    for c in copies:
+        c.start()
+    for c in copies:
+        c.wait()
 
 
 def local(tokens, output_grad, router, weight_in, weight_out):
@@ -493,10 +482,10 @@
     dma = pltpu.SemaphoreType.DMA
     vm = pl.BlockSpec(memory_space=pltpu.VMEM)
     hbm = pl.BlockSpec(memory_space=pl.ANY)
-    land, rg = pl.pallas_call(
+    tg, rg = pl.pallas_call(
         kernel,
         name="moe_backward",
-        out_shape=(pltpu.VMEM((4, PAD, 256), BF), pltpu.VMEM((16, S), F32)),
+        out_shape=(pltpu.VMEM((TOK * 8, 128), BF), pltpu.VMEM((16, S), F32)),
         in_specs=[hbm, hbm, hbm, hbm, hbm],
         out_specs=(vm, vm),
         scratch_shapes=[
@@ -505,6 +494,7 @@
             pltpu.VMEM((PAD, D), BF),
             pltpu.VMEM((PAD, D), BF),
             pltpu.VMEM((D, S), BF),
+            pltpu.VMEM((4, PAD, 256), BF),
             pltpu.VMEM((2, D, D), BF),
             pltpu.VMEM((2, D, D), BF),
             pltpu.VMEM((PAD, S), F32),
@@ -536,16 +526,16 @@
             pltpu.VMEM((4, 8, 128), F32),
             dma((2, 4)),
             dma((3,)),
-            dma((4,)), dma((4, 2)),
-            dma((4, 2)), dma((4, 2)),
-            dma((4, 2, 2)), dma((4, 2, 2)),
-            dma((4, 2)), dma((4, 2)),
-            dma((4, 2)), dma((4, 2)),
-            dma((4,)), dma((2,)),
+            dma, dma((4, 2)),
+            dma, dma((4, 2)),
+            dma, dma((4, 2)),
+            dma, dma((4, 2)),
+            dma, dma((4, 2)),
+            dma, dma((2,)),
             dma, dma,
             dma, dma,
-            dma((4,)), dma((4,)),
-            dma((4,)), dma((4,)),
+            dma, dma,
+            dma, dma,
         ],
         compiler_params=pltpu.CompilerParams(
             collective_id=0, has_side_effects=True, vmem_limit_bytes=58 * 1024 * 1024
@@ -559,10 +549,10 @@
             jax.ShapeDtypeStruct((16, S), F32),
         ),
         in_specs=[vm, vm],
-        out_specs=(vm, vm),
-        scratch_shapes=[pltpu.VMEM((PAD * 8, 128), F32)],
-        compiler_params=pltpu.CompilerParams(vmem_limit_bytes=16 * 1024 * 1024),
-    )(land, rg)
+        out_specs=(hbm, hbm),
+        scratch_shapes=[dma((5,))],
+        compiler_params=pltpu.CompilerParams(vmem_limit_bytes=8 * 1024 * 1024),
+    )(tg, rg)
     tg = tg.reshape(TOK, 2, 4, 128).transpose(2, 0, 1, 3).reshape(4, TOK, 256)
     return tg, rg
 

time: 67.6 us -> 65.9 us (0.975)
  Pallas kernels: 66.5 us -> 65.2 us
    pallas_call x1, Pallas kernels: 65.5 us -> 64.4 us  [local(): pl.pallas_call(kernel, name='moe_backward', out_shape=(pltpu.VMEM((TOK *...]
where the time goes in v4:
time: 65.9 us; the launch traced here: 65.8 us
  Pallas kernels  65.2 us (99%)
    pallas_call x1, Pallas kernels, local(): pl.pallas_call(kernel, name='moe_backward', out_shape=(pltpu.VMEM((TOK *...  64.4 us

profile of v4, /device:TPU:1, one launch (start us, length us, event | category | flops | bytes accessed | tf_op | source)
XLA Modules:
  0.0 65.8 jit_solution(2460166088015210698)
XLA Ops:
  0.6 64.4 %moe_backward.1 = (bf16[1568,128]{1,0:T(8,128)(2,1)S(1)}, f32[16,128]{1,0:T(8,128)S(1)}) custom-call(bf16[6272,128]{1,0:T(8,128)(2,1)} %bitcast.19, bf16[6272,128]{1,0:T(8,128)(2,1)} %bitcast.20, bf16[1024,128]{1,0:T(8,128)(2,1)} %router_all.1, bf16[2,1024,1024]{2,1,0:T(8,128)(2,1)} %w_in.1, bf16[2,1024,1024]{2,1,0:T(8,128)(2,1)} %w_out.1), custom_call_target="tpu_custom_call" | custom-call | tf_op jit(solution)/shard_map/moe_backward/pallas_call | solution.py:485
  65.0 0.8 %moe_finish.1 = (bf16[1568,128]{1,0:T(8,128)(2,1)}, f32[16,128]{1,0:T(8,128)}) custom-call(bf16[1568,128]{1,0:T(8,128)(2,1)S(1)} %get-tuple-element.6.tg, f32[16,128]{1,0:T(8,128)S(1)} %get-tuple-element.7.rg), custom_call_target="tpu_custom_call" | custom-call | tf_op jit(solution)/shard_map/moe_finish/pallas_call | solution.py:544

commit v5 on v4

--- a/solution.py
+++ b/solution.py
@@ -34,7 +34,7 @@
 def kernel(
     tok_all, og_all, router_all, w_in, w_out,
     tg_out, rg,
-    raw, wide, tok, og, router, land, win, wout, disp, comb, sbuf, x, fs, lhs, dg, act, pg, s0, s1, s2, s3,
+    raw, wide, tok, og, router, land, tok_t, win, wout, disp, comb, sbuf, x, fs, lhs, dg, act, pg, s0, s1, s2, s3,
     cbuf, pbuf, ybuf, rbuf, abuf, so, so_m, rgo, rgs, rgp, rgb, rr, tgb, qs,
     tsem, wsem, send1, recv1, ysend, yrecv, csend, crecv,
     psend, precv, bsend, brecv, asend, arecv,
@@ -51,7 +51,7 @@
     ahead = [lax.rem(zc + dz, NZ) * NY for dz in range(NZ)]
     behind = [lax.rem(zc + NZ - dz, NZ) * NY for dz in range(NZ)]
 
-    def each_peer(fn, half, back=False):
+    def each_peer(fn, half, back=False, down=False):
         def at(t, js):
             dx, dy = lax.rem(t, NX), lax.div(t, NX)
             x2 = lax.rem(xc + (NX - dx if back else dx), NX) * (NY * NZ)
@@ -68,7 +68,7 @@
 
         @pl.loop(lo, 8)
         def _(t):
-            at(t, (0, 1, 2, 3))
+            at(lo + 7 - t if down else t, (0, 1, 2, 3))
 
     def quad(j):
         return lax.rem(yl + j // 2, 2) * 2 + lax.rem(core + j % 2, 2)
@@ -92,8 +92,8 @@
     def greet(i2, g2, r):
         pl.semaphore_signal(barrier, inc=1, device_id=dev(g2, i2))
 
-    each_peer(greet, FAR)
-    each_peer(greet, NEAR)
+    each_peer(greet, FAR, down=True)
+    each_peer(greet, NEAR, down=True)
     for j in range(1, 4):
         pl.semaphore_signal(barrier, inc=1, device_id=dev(quad(j), inner))
 
@@ -171,7 +171,7 @@
 
     def ccopy(st, q, h):
         return pltpu.make_async_remote_copy(
-            part(st, q, h), part(st, q + 2, h), csend, crecv.at[st, q],
+            part(st, q, h), part(st, q + 2, h), csend, crecv.at[st],
             device_id=dev(quad(1), inner),
         )
 
@@ -198,10 +198,10 @@
         to_rows(st, 1)
 
     def rows_cd(st):
+        with scope(f"settle{st}"):
+            done = x.at[st, pl.ds(2, 2)]
+            pltpu.make_async_copy(done, done, crecv.at[st]).wait()
         for q in range(2):
-            with scope(f"settle{st}{q}"):
-                done = x.at[st, q + 2]
-                pltpu.make_async_copy(done, done, crecv.at[st, q]).wait()
             to_rows(st, q + 2)
 
     def scatter_rows(dst, n, val):
@@ -267,10 +267,11 @@
                 )
                 pcopy(st, q).start()
 
-    def reduce_2(st):
+    def reduce_2(st, halves=(FAR, NEAR), first=True):
         with scope(f"reduce2_{st}"):
-            pcopy(st, 1).wait_recv()
-            for h in (FAR, NEAR):
+            if first:
+                pcopy(st, 1).wait_recv()
+            for h in halves:
                 sel = pl.ds(h * 32, 32)
                 ybuf[st, sel] = (rows_of(st, 1, h) + pbuf[st, 1, sel].astype(F32)).astype(BF)
                 bcopy(st, h).start()
@@ -299,6 +300,13 @@
         with scope("a2a"):
             each_peer(send, h, back=True)
 
+    with scope("tok_t"):
+        for a in range(8):
+            turned = tok[:, a * 128 : (a + 1) * 128].astype(F32).T.reshape(8, 2, 8, PAD)
+            for half in range(2):
+                tok_t[half, a * 64 : (a + 1) * 64, :] = (
+                    turned[:, half].reshape(64, PAD).astype(BF)
+                )
     forward_a(0, NEAR)
     forward_a(0, FAR)
     forward_a(1, NEAR)
@@ -379,13 +387,12 @@
     dw = disp[...]
     lg = lg + dw * (dgr - jnp.sum(dw * dgr, axis=0, keepdims=True))
     lb = lg.astype(BF)
-    rgo[...] = dot(tok[...], lb, 0, 0).reshape(NI, 2, 8, 128)
-    rgs[...] = rgo[:, pl.ds(1 - core, 1)].reshape(NI, 8, 128).astype(BF)
-
+    rgs[...] = dot(tok_t[1 - core], lb, 1, 0).reshape(NI, 8, 128).astype(BF)
     gcopy = pltpu.make_async_remote_copy(
         rgs, rgp, gsend, grecv, device_id=dev(quad(1), inner)
     )
     gcopy.start()
+    rgo[...] = dot(tok_t[core], lb, 1, 0).reshape(NI, 8, 128)
     with scope("tg"):
         tg = dot(dw.astype(BF), so_m[1], 1, 0) + dot(lb, router[...], 1, 1)
         for g in range(4):
@@ -404,9 +411,7 @@
 
     with scope("wait_g"):
         gcopy.wait_recv()
-    rgb[...] = (
-        rgo[:, pl.ds(core, 1)].reshape(NI, 8, 128) + rgp[...].astype(F32)
-    ).astype(BF)
+    rgb[...] = (rgo[...] + rgp[...].astype(F32)).astype(BF)
 
     def send_router(i2, g2, r):
         pltpu.make_async_remote_copy(
@@ -495,6 +500,7 @@
             pltpu.VMEM((PAD, D), BF),
             pltpu.VMEM((D, S), BF),
             pltpu.VMEM((4, PAD, 256), BF),
+            pltpu.VMEM((2, D // 2, PAD), BF),
             pltpu.VMEM((2, D, D), BF),
             pltpu.VMEM((2, D, D), BF),
             pltpu.VMEM((PAD, S), F32),
@@ -517,7 +523,7 @@
             pltpu.VMEM((4, NI, 8, 128), BF),
             pltpu.VMEM((2, NI, 2, 8, 128), BF),
             pltpu.VMEM((2, S, D), BF),
-            pltpu.VMEM((NI, 2, 8, 128), F32),
+            pltpu.VMEM((NI, 8, 128), F32),
             pltpu.VMEM((NI, 8, 128), BF),
             pltpu.VMEM((NI, 8, 128), BF),
             pltpu.VMEM((NI, 8, 128), BF),
@@ -528,7 +534,7 @@
             dma((3,)),
             dma, dma((4, 2)),
             dma, dma((4, 2)),
-            dma, dma((4, 2)),
+            dma, dma((4,)),
             dma, dma((4, 2)),
             dma, dma((4, 2)),
             dma, dma((2,)),

time: 65.9 us -> 65.7 us (level)
  no operation moved by 1% of the time
where the time goes in v5:
time: 65.7 us; the launch traced here: 65.6 us
  Pallas kernels  65 us (99%)
    pallas_call x1, Pallas kernels, local(): pl.pallas_call(kernel, name='moe_backward', out_shape=(pltpu.VMEM((TOK *...  64.2 us

profile of v5, /device:TPU:1, one launch (start us, length us, event | category | flops | bytes accessed | tf_op | source)
XLA Modules:
  0.0 65.6 jit_solution(17215488726615411015)
XLA Ops:
  0.6 64.2 %moe_backward.1 = (bf16[1568,128]{1,0:T(8,128)(2,1)S(1)}, f32[16,128]{1,0:T(8,128)S(1)}) custom-call(bf16[6272,128]{1,0:T(8,128)(2,1)} %bitcast.19, bf16[6272,128]{1,0:T(8,128)(2,1)} %bitcast.20, bf16[1024,128]{1,0:T(8,128)(2,1)} %router_all.1, bf16[2,1024,1024]{2,1,0:T(8,128)(2,1)} %w_in.1, bf16[2,1024,1024]{2,1,0:T(8,128)(2,1)} %w_out.1), custom_call_target="tpu_custom_call" | custom-call | tf_op jit(solution)/shard_map/moe_backward/pallas_call | solution.py:490
  64.8 0.8 %moe_finish.1 = (bf16[1568,128]{1,0:T(8,128)(2,1)}, f32[16,128]{1,0:T(8,128)}) custom-call(bf16[1568,128]{1,0:T(8,128)(2,1)S(1)} %get-tuple-element.6.tg, f32[16,128]{1,0:T(8,128)S(1)} %get-tuple-element.7.rg), custom_call_target="tpu_custom_call" | custom-call | tf_op jit(solution)/shard_map/moe_finish/pallas_call | solution.py:550

commit v6 on v5

--- a/solution.py
+++ b/solution.py
@@ -157,7 +157,7 @@
         pl.semaphore_wait(barrier, NI - 1 + 3)
     with scope("send"):
         for st in range(4):
-            for h in (NEAR, FAR) if st == 0 else (FAR, NEAR):
+            for h in (NEAR, FAR) if st < 3 else (FAR, NEAR):
                 send_stage(st, h)
 
     def part(st, q, h):
@@ -355,9 +355,9 @@
     with scope("rows"):
         rows_ab(3)
         rows_cd(3)
-    reduce_3(0, FAR)
     with scope("actgrad"):
         act_grad(1)
+    reduce_3(0, FAR)
     reduce_2(2)
     reduce_3(0, NEAR)
     with scope("back"):

time: 65.7 us -> 66.6 us (1.014)
  Pallas kernels: 65 us -> 65.9 us
    pallas_call x1, Pallas kernels: 64.2 us -> 65.1 us  [local(): pl.pallas_call(kernel, name='moe_backward', out_shape=(pltpu.VMEM((TOK *...]
where the time goes in v6:
time: 66.6 us
  Pallas kernels  65.9 us (99%)
    pallas_call x1, Pallas kernels, local(): pl.pallas_call(kernel, name='moe_backward', out_shape=(pltpu.VMEM((TOK *...  65.1 us

profile of v6, /device:TPU:1, one launch (start us, length us, event | category | flops | bytes accessed | tf_op | source)
XLA Modules:
  0.0 66.6 jit_solution(9034381807656645326)
XLA Ops:
  0.6 65.1 %moe_backward.1 = (bf16[1568,128]{1,0:T(8,128)(2,1)S(1)}, f32[16,128]{1,0:T(8,128)S(1)}) custom-call(bf16[6272,128]{1,0:T(8,128)(2,1)} %bitcast.19, bf16[6272,128]{1,0:T(8,128)(2,1)} %bitcast.20, bf16[1024,128]{1,0:T(8,128)(2,1)} %router_all.1, bf16[2,1024,1024]{2,1,0:T(8,128)(2,1)} %w_in.1, bf16[2,1024,1024]{2,1,0:T(8,128)(2,1)} %w_out.1), custom_call_target="tpu_custom_call" | custom-call | tf_op jit(solution)/shard_map/moe_backward/pallas_call | solution.py:490
  65.8 0.8 %moe_finish.1 = (bf16[1568,128]{1,0:T(8,128)(2,1)}, f32[16,128]{1,0:T(8,128)}) custom-call(bf16[1568,128]{1,0:T(8,128)(2,1)S(1)} %get-tuple-element.6.tg, f32[16,128]{1,0:T(8,128)S(1)} %get-tuple-element.7.rg), custom_call_target="tpu_custom_call" | custom-call | tf_op jit(solution)/shard_map/moe_finish/pallas_call | solution.py:550
